TPU v7x, 32 devices: a whole 2x2x4 slice. The times are simulated.
32 devices in a mesh: tgt: 16 (over z, y, x), src: 2 (over core).
Axes of the slice: x: 2, y: 2, z: 4, core: 2. Of those that a mesh axis runs over, the one named last changes fastest.
Arguments:
- node_feats: bfloat16 [4096, 128], P(('tgt', 'src')), may hold values from -6 to 6
- tile_index: int32 [16, 2, 8], P('tgt', 'src'), may hold values from 0 to 31, as said below
- tile_count: int32 [16, 2], P('tgt', 'src'), may hold values from 1 to 8
- tile_vals: float32 [16, 2, 8, 128, 128], P('tgt', 'src'), may hold values from -0.375 to 0.375
- w_in: bfloat16 [128, 512], replicated, may hold values from -0.5 to 0.5
- w_out: bfloat16 [512, 172], replicated, may hold values from -0.25 to 0.25
Outputs:
- logits: float32 [4096, 172], P(('tgt', 'src'))
Inputs may be any that keep to these rules, and one draw needn't show every extreme that they name: `tile_index`: within one block pair the slots' entries are distinct.
All inputs are finite; a program needn't handle non-finite values.
Results may differ from a plain program's by a relative error of at most 0.005.
Values may be sent and summed in bfloat16 or wider, within the bound.
No kernel may reach another device: no remote copies, remote signals or barrier semaphores. Data moves between devices by JAX's collectives and lax.ppermute only.
A program may use at most 64 MiB of HBM per device.

v0:
```python
import functools

import jax
import jax.numpy as jnp
from jax import lax
from jax.experimental import pallas as pl
from jax.experimental.pallas import tpu as pltpu
from jax.sharding import PartitionSpec as P


VMEM = pl.BlockSpec(memory_space=pltpu.VMEM)
SMEM = pl.BlockSpec(memory_space=pltpu.SMEM)
GRANT = pltpu.CompilerParams(vmem_limit_bytes=24 << 20)
DIRECT = 4
CFG = {"p": ((3, 2, 1), {2: 1}, (3, 1, 2)), "s": ((3, 2, 1), {3: 1, 2: 2}, (3, 1, 2))}
EARLY, MIDDLE, LATE = ((0, True), (1, False), (2, False), (3, False)), ((3, True),), ((1, True), (2, True))


def inside(*arrays):
    return [pltpu.with_memory_space_constraint(array, pltpu.VMEM) for array in arrays]


def place_kernel(row_tiles, code_ref, tiles_ref, w_in_ref, high_ref, low_ref, w_in_t_ref):
    slots, tile, _ = tiles_ref.shape
    for slot in range(slots):
        values = tiles_ref[slot]
        high = values.astype(jnp.bfloat16).astype(jnp.float32)
        low = values - high
        code = jnp.full((tile, tile), code_ref[slot], jnp.int32)
        columns = slice(slot * tile, (slot + 1) * tile)
        for row in range(row_tiles):
            rows = slice(row * tile, (row + 1) * tile)
            here = code == row
            high_ref[rows, columns] = jnp.where(here, high, 0.0).astype(jnp.bfloat16)
            low_ref[rows, columns] = jnp.where(here, low, 0.0).astype(jnp.bfloat16)
    w_in_t_ref[...] = w_in_ref[...].T


def pick(spot_ref, pieces, joined_ref, picked_ref, tile):
    base = 0
    for piece in pieces:
        joined_ref[base : base + piece.shape[0], :] = piece[...]
        base += piece.shape[0]
    for slot in range(picked_ref.shape[0] // tile):
        start = pl.multiple_of(spot_ref[slot] * tile, tile)
        picked_ref[slot * tile : (slot + 1) * tile, :] = joined_ref[pl.ds(start, tile), :]


def rows_times(high_ref, low_ref, rows, columns, picked):
    return jnp.dot(high_ref[rows, columns], picked, preferred_element_type=jnp.float32) + jnp.dot(
        low_ref[rows, columns], picked, preferred_element_type=jnp.float32
    )


def times_transposed(left, right):
    return lax.dot_general(left, right, (((1,), (1,)), ((), ())), preferred_element_type=jnp.float32)


def times_rows(message, high_ref, low_ref, rows, columns):
    return times_transposed(message, high_ref[rows, columns]) + times_transposed(message, low_ref[rows, columns])


def transform(agg, w_in_t_ref, w_out_t_ref):
    hidden = jnp.maximum(times_transposed(w_in_t_ref[...], agg), 0.0).astype(jnp.bfloat16)
    return jnp.dot(w_out_t_ref[...], hidden, preferred_element_type=jnp.float32).astype(jnp.bfloat16)


def first_kernel(count, tile, spot_ref, high_ref, low_ref, *refs):
    pieces, outs, (joined_ref, picked_ref) = refs[:count], refs[count:-2], refs[-2:]
    pick(spot_ref, pieces, joined_ref, picked_ref, tile)
    picked, own = picked_ref[...], outs[0].shape[0]
    for d, out in enumerate(outs):
        out[...] = rows_times(high_ref, low_ref, slice(d * own, (d + 1) * own), slice(None), picked)


def second_kernel(count, tile, spot_ref, high_ref, low_ref, w_in_t_ref, w_out_t_ref, *refs):
    pieces, outs, (joined_ref, picked_ref) = refs[:count], refs[count:-2], refs[-2:]
    pick(spot_ref, pieces, joined_ref, picked_ref, tile)
    message = transform(picked_ref[...], w_in_t_ref, w_out_t_ref)
    own = outs[0].shape[1]
    for d, out in enumerate(outs):
        out[...] = times_rows(message, high_ref, low_ref, slice(d * own, (d + 1) * own), slice(None))


def place_dense_kernel(code_ref, spot_ref, tiles_ref, w_in_ref, high_ref, low_ref, w_in_t_ref):
    slots, tile, _ = tiles_ref.shape
    high_ref[...] = jnp.zeros_like(high_ref)
    low_ref[...] = jnp.zeros_like(low_ref)
    for slot in range(slots):

        @pl.when(code_ref[slot] >= 0)
        def _(slot=slot):
            values = tiles_ref[slot]
            high = values.astype(jnp.bfloat16)
            rows = pl.ds(pl.multiple_of(code_ref[slot] * tile, tile), tile)
            columns = pl.ds(pl.multiple_of(spot_ref[slot] * tile, tile), tile)
            high_ref[rows, columns] = high
            low_ref[rows, columns] = (values - high.astype(jnp.float32)).astype(jnp.bfloat16)

    w_in_t_ref[...] = w_in_ref[...].T


def first_dense_kernel(spans, rows, summed, high_ref, low_ref, *refs):
    before, pieces, out_ref = refs[:summed], refs[summed:-1], refs[-1]
    total = before[0][rows, :] if summed else None
    for columns, piece in zip(spans, pieces):
        term = rows_times(high_ref, low_ref, rows, columns, piece[...])
        total = term if total is None else total + term
    out_ref[...] = total


def second_dense_kernel(spans, own, summed, high_ref, low_ref, w_in_t_ref, w_out_t_ref, *refs):
    count = len(spans)
    before, pieces, outs = refs[:summed], refs[summed : summed + count], refs[summed + count :]
    message = transform(jnp.concatenate([piece[...] for piece in pieces], 0), w_in_t_ref, w_out_t_ref)
    total = before[0][...] if summed else None
    base = 0
    for columns in spans:
        size = columns.stop - columns.start
        term = times_rows(message[:, base : base + size], high_ref, low_ref, slice(None), columns)
        total = term if total is None else total + term
        base += size
    for d, out in enumerate(outs):
        out[...] = total[:, d * own : d * own + out.shape[1]]


def hop(value, groups, bits):
    pairs = [(group[i], group[i ^ bits]) for group in groups for i in range(len(group))]
    return lax.ppermute(value, "tgt", pairs)


def gather(value, groups):
    whole = lax.all_gather(value, "tgt", axis=0, axis_index_groups=groups)
    return [whole[i] for i in range(len(groups[0]))]


def spread(value, inner, outer, name):
    across = [[o * inner + i for o in range(outer)] for i in range(inner)]
    within = [[o * inner + i for i in range(inner)] for o in range(outer)]
    if not by_hops(inner, outer):
        return gather(jnp.concatenate(gather(value, across), 0), within)
    blocks = [value] + [hop(value, across, bits) for bits in (3, 2, 1)]
    column = jnp.concatenate(blocks, 0)
    pieces = [column]
    for bits in range(1, inner):
        split = CFG[name][1].get(bits, 0)
        if split:
            parts = [jnp.concatenate(part, 0) if len(part) > 1 else part[0] for part in (blocks[:split], blocks[split:])]
            pieces.append((hop(parts[0], within, bits), hop(parts[1], within, bits)))
        else:
            pieces.append(hop(column, within, bits))
    return pieces


def to_owner(parts, n_src):
    moved = []
    for d, part in enumerate(parts, 1):
        pairs = [(i, (i + d) % n_src) for i in range(n_src)]
        moved.append(lax.ppermute(part, "src", pairs))
    return moved


def factors(n_tgt):
    inner = 1 << ((n_tgt.bit_length() - 1) // 2)
    return inner, n_tgt // inner


def by_hops(inner, outer):
    return inner == outer == DIRECT


def layers(node_feats, tile_index, tile_count, tile_vals, w_in, w_out):
    tiles = tile_vals[0, 0]
    slots, tile, _ = tiles.shape
    own, width = node_feats.shape
    hidden_size, classes = w_out.shape
    n_src, n_tgt = lax.axis_size("src"), lax.axis_size("tgt")
    row_tiles, col_tiles = own * n_src // tile, own * n_tgt // tile
    per_own = own // tile
    inner, outer = factors(n_tgt)

    index, count = tile_index[0, 0], tile_count[0, 0]
    mine_t, mine_s = lax.axis_index("tgt"), lax.axis_index("src")
    turned = (index // col_tiles + row_tiles - mine_s * per_own) % row_tiles
    code = jnp.where(jnp.arange(slots) < count, turned, -1).astype(jnp.int32)
    column = index % col_tiles
    node, part = column // per_own, column % per_own
    in_spot, out_spot = node % inner, node // inner
    if by_hops(inner, outer):
        in_spot, out_spot = in_spot ^ (mine_t % inner), (outer - (out_spot ^ (mine_t // inner))) % outer
    spot = ((in_spot * outer + out_spot) * per_own + part).astype(jnp.int32)

    def call(kernel, outs, n_small, args, scratch=(), flops=0):
        return pl.pallas_call(
            kernel,
            out_shape=outs,
            in_specs=[SMEM] * n_small + [VMEM] * (len(args) - n_small),
            out_specs=jax.tree.map(lambda _: VMEM, outs),
            scratch_shapes=scratch,
            compiler_params=GRANT,
            cost_estimate=pl.CostEstimate(flops=flops, bytes_accessed=1 << 20, transcendentals=0),
        )(*args[:n_small], *inside(*args[n_small:]))

    all_rows, agg_part = row_tiles * tile, pltpu.VMEM((own, width), jnp.float32)
    out_part = pltpu.VMEM((classes, own), jnp.float32)
    w_in_shape, w_out_t = pltpu.VMEM(w_in.shape[::-1], w_in.dtype), w_out.T
    weights = 2 * (width * hidden_size + hidden_size * classes)
    pieces = spread(node_feats, inner, outer, "p")

    if by_hops(inner, outer):
        placed = pltpu.VMEM((all_rows, own * n_tgt), jnp.bfloat16)
        high, low, w_in_t = call(place_dense_kernel, [placed, placed, w_in_shape], 2, (code, spot, tiles, w_in))

        def pick_pieces(group):
            held, spans = [], []
            for number, late in group:
                parts = pieces[number] if isinstance(pieces[number], tuple) else (pieces[number],)
                base = number * own * outer
                for i, part in enumerate(parts):
                    if i == len(parts) - 1 if late else i < len(parts) - 1:
                        held.append(part)
                        spans.append(slice(base, base + part.shape[0]))
                    base += part.shape[0]
            return held, spans

        def first(numbers, rows, before):
            held, spans = pick_pieces(numbers)
            kernel = functools.partial(first_dense_kernel, spans, rows, len(before))
            size = rows.stop - rows.start
            return call(
                kernel,
                pltpu.VMEM((size, width), jnp.float32),
                0,
                (high, low, *before, *held),
                (),
                4 * size * own * outer * width,
            )

        every = slice(0, all_rows)
        early = first(EARLY, every, ())
        early = first(MIDDLE, every, (early,))
        others = [first(LATE, slice(d * own, (d + 1) * own), (early,)) for d in range(1, n_src)]
        moved = to_owner(others, n_src)
        mine = first(LATE, slice(0, own), (early,))
    else:
        depth = slots * tile
        placed = pltpu.VMEM((all_rows, depth), jnp.bfloat16)
        high, low, w_in_t = call(functools.partial(place_kernel, row_tiles), [placed, placed, w_in_shape], 1, (code, tiles, w_in))
        scratch = [pltpu.VMEM((own * n_tgt, width), jnp.bfloat16), pltpu.VMEM((depth, width), jnp.bfloat16)]
        mine, *others = call(
            functools.partial(first_kernel, len(pieces), tile),
            [agg_part] * n_src,
            1,
            (spot, high, low, *pieces),
            scratch,
            4 * all_rows * depth * width,
        )
        moved = to_owner(others, n_src)
    agg = sum(moved, mine).astype(jnp.bfloat16)

    pieces = spread(agg, inner, outer, "s")
    if by_hops(inner, outer):

        def second(numbers, before, last):
            held, spans = pick_pieces(numbers)
            kernel = functools.partial(second_dense_kernel, spans, own, len(before))
            return call(
                kernel,
                [out_part] * n_src if last else [pltpu.VMEM((classes, all_rows), jnp.float32)],
                0,
                (high, low, w_in_t, w_out_t, *before, *held),
                (),
                own * outer * (weights + 4 * all_rows * classes),
            )

        early = second(EARLY, (), False)
        early = second(MIDDLE, early, False)
        mine, *others = second(LATE, early, True)
    else:
        mine, *others = call(
            functools.partial(second_kernel, len(pieces), tile),
            [out_part] * n_src,
            1,
            (spot, high, low, w_in_t, w_out_t, *pieces),
            scratch,
            depth * (weights + 4 * all_rows * classes),
        )
    return sum(to_owner(others, n_src), mine).T


def solution(mesh):
    in_specs = (
        P(("tgt", "src"), None),
        P("tgt", "src", None),
        P("tgt", "src"),
        P("tgt", "src", None, None, None),
        P(),
        P(),
    )
    out_specs = P(("tgt", "src"), None)
    return jax.shard_map(layers, mesh=mesh, in_specs=in_specs, out_specs=out_specs, check_vma=False)
```

profile of v0, /device:TPU:0, one launch (start us, length us, event | category | flops | bytes accessed | tf_op | source)
XLA Modules:
  0.0 40.0 jit_solution(10497344076647379611)
XLA Ops:
  0.0 5.1 %collective-permute-start = (bf16[128,128]{1,0:T(8,128)(2,1)}, bf16[128,128]{1,0:T(8,128)(2,1)S(1)}, u32[]{:S(2)}, u32[]{:S(2)}) collective-permute-start(bf16[128,128]{1,0:T(8,128)(2,1)} %param.6), channel_id=1, source_target_pairs={{0,24},{8,16},{16,8},{24,0},{2,26},{10,18},{18,10},{26,2},{4,28},{... | collective-permute-start | bytes 98312 | tf_op jit(solution)/shard_map/ppermute | solution.py:129
  5.1 0.0 collective-permute-start.1
  5.1 0.6 %collective-permute-start.2 = (bf16[128,128]{1,0:T(8,128)(2,1)}, bf16[128,128]{1,0:T(8,128)(2,1)S(1)}, u32[]{:S(2)}, u32[]{:S(2)}) collective-permute-start(bf16[128,128]{1,0:T(8,128)(2,1)} %param.6), channel_id=1, source_target_pairs={{0,8},{8,0},{16,24},{24,16},{2,10},{10,2},{18,26},{26,18},{4,12},{... | collective-permute-start | bytes 98312 | tf_op jit(solution)/shard_map/ppermute | solution.py:129
  5.6 1.7 %collective-permute-start.3 = (bf16[128,128]{1,0:T(8,128)(2,1)}, bf16[128,128]{1,0:T(8,128)(2,1)S(1)}, u32[]{:S(2)}, u32[]{:S(2)}) collective-permute-start(bf16[128,128]{1,0:T(8,128)(2,1)} %param.6), channel_id=1, source_target_pairs={{0,4},{2,6},{4,0},{6,2},{8,12},{10,14},{12,8},{14,10},{16,20},{18,... | collective-permute-start | bytes 98312 | tf_op jit(solution)/shard_map/ppermute | solution.py:129
  7.4 0.8 %constant_dynamic-update-slice_fusion.3 = bf16[512,128]{1,0:T(8,128)(2,1)S(1)} fusion(bf16[128,128]{1,0:T(8,128)(2,1)} %param.6), kind=kLoop, calls=%fused_computation.10 | loop fusion | bytes 65536
  8.8 0.0 collective-permute-done
  8.9 1.2 %collective-permute-done.1 = bf16[128,128]{1,0:T(8,128)(2,1)S(1)} collective-permute-done((bf16[128,128]{1,0:T(8,128)(2,1)}, bf16[128,128]{1,0:T(8,128)(2,1)S(1)}, u32[]{:S(2)}, u32[]{:S(2)}) %collective-permute-start.1) | collective-permute-done | bytes 32800 | tf_op jit(solution)/shard_map/ppermute | solution.py:129
  10.1 0.0 copy-start.2
  10.1 0.0 collective-permute-done.2
  10.1 2.5 %collective-permute-start.4 = (bf16[512,128]{1,0:T(8,128)(2,1)S(1)}, bf16[512,128]{1,0:T(8,128)(2,1)S(1)}, u32[]{:S(2)}, u32[]{:S(2)}) collective-permute-start(bf16[512,128]{1,0:T(8,128)(2,1)S(1)} %constant_dynamic-update-slice_fusion.refs_0_), channel_id=1, source_target_pairs={{0,6},{2,4},{4,2},{6,0},{8,14},{10,12},{12,10},{14,8},{16,22},{18,... | collective-permute-start | bytes 393224 | tf_op jit(solution)/shard_map/ppermute | solution.py:129
  12.7 0.5 %collective-permute-start.5 = (bf16[512,128]{1,0:T(8,128)(2,1)S(1)}, bf16[512,128]{1,0:T(8,128)(2,1)S(1)}, u32[]{:S(2)}, u32[]{:S(2)}) collective-permute-start(bf16[512,128]{1,0:T(8,128)(2,1)S(1)} %constant_dynamic-update-slice_fusion.refs_0_), channel_id=1, source_target_pairs={{0,2},{2,0},{4,6},{6,4},{8,10},{10,8},{12,14},{14,12},{16,18},{18,... | collective-permute-start | bytes 393224 | tf_op jit(solution)/shard_map/ppermute | solution.py:129
  13.2 0.0 copy-start.3
  13.2 0.6 %collective-permute-start.6 = (bf16[384,128]{1,0:T(8,128)(2,1)S(1)}, bf16[384,128]{1,0:T(8,128)(2,1)S(1)}, u32[]{:S(2)}, u32[]{:S(2)}) collective-permute-start(bf16[384,128]{1,0:T(8,128)(2,1)S(1)} %pad_maximum_fusion.1), channel_id=1, source_target_pairs={{0,4},{2,6},{4,0},{6,2},{8,12},{10,14},{12,8},{14,10},{16,20},{18,... | collective-permute-start | bytes 294920 | tf_op jit(solution)/shard_map/ppermute | solution.py:129
  13.8 0.1 copy-done.3
  13.9 0.0 copy-done.2
  13.9 0.0 copy-start.1
  13.9 1.0 %copy-done.1 = f32[1,1,8,128,128]{4,3,2,1,0:T(8,128)S(1)} copy-done((f32[1,1,8,128,128]{4,3,2,1,0:T(8,128)S(1)}, f32[1,1,8,128,128]{4,3,2,1,0:T(8,128)}, u32[]{:S(2)}) %copy-start.1) | copy-done | bytes 524312
  14.9 0.9 %shard_map.64 = (bf16[256,2048]{1,0:T(8,128)(2,1)S(1)}, bf16[256,2048]{1,0:T(8,128)(2,1)S(1)}, bf16[512,128]{1,0:T(8,128)(2,1)S(1)}) custom-call(s32[8]{0:T(128)S(1)} %get-tuple-element.16.code_ref, s32[8]{0:T(128)S(1)} %get-tuple-element.15.spot_ref, f32[8,128,128]{2,1,0:T(8,128)S(1)} %bitcast.26, bf16[128,512]{1,0:T(8,128)(2,1)S(1)} %copy-done.2), custom_call_target="tpu_custom_call" | custom-call | bytes 1048576 | tf_op jit(solution)/shard_map/pallas_call | solution.py:194
  15.9 0.0 collective-permute-done.3.refs_1_
  15.9 0.3 shard_map.65.refs_0_
  16.2 0.1 collective-permute-done.4.refs_1_
  16.3 0.3 shard_map.66.refs_0_
  16.6 1.3 %collective-permute-done.6.refs_2_ = bf16[384,128]{1,0:T(8,128)(2,1)S(1)} collective-permute-done((bf16[384,128]{1,0:T(8,128)(2,1)S(1)}, bf16[384,128]{1,0:T(8,128)(2,1)S(1)}, u32[]{:S(2)}, u32[]{:S(2)}) %collective-permute-start.6) | collective-permute-done | bytes 98336 | tf_op jit(solution)/shard_map/ppermute | solution.py:129
  17.9 0.0 collective-permute-done.5.refs_1_
  17.9 0.3 shard_map.68
  18.2 0.1 collective-permute-start.7
  18.3 0.3 shard_map.67
  18.5 1.0 %collective-permute-done.7 = f32[128,128]{1,0:T(8,128)S(1)} collective-permute-done((f32[128,128]{1,0:T(8,128)S(1)}, f32[128,128]{1,0:T(8,128)S(1)}, u32[]{:S(2)}, u32[]{:S(2)}) %collective-permute-start.7) | collective-permute-done | bytes 65568 | tf_op jit(solution)/shard_map/ppermute | solution.py:159
  19.5 0.2 collective-permute-start.10
  19.7 2.6 %collective-permute-start.9 = (bf16[128,128]{1,0:T(8,128)(2,1)S(1)}, bf16[128,128]{1,0:T(8,128)(2,1)S(1)}, u32[]{:S(2)}, u32[]{:S(2)}) collective-permute-start(bf16[128,128]{1,0:T(8,128)(2,1)S(1)} %add_convert_fusion), channel_id=1, source_target_pairs={{0,16},{8,24},{16,0},{24,8},{2,18},{10,26},{18,2},{26,10},{4,20},{... | collective-permute-start | bytes 98312 | tf_op jit(solution)/shard_map/ppermute | solution.py:129
  22.3 1.6 %collective-permute-start.8 = (bf16[128,128]{1,0:T(8,128)(2,1)S(1)}, bf16[128,128]{1,0:T(8,128)(2,1)S(1)}, u32[]{:S(2)}, u32[]{:S(2)}) collective-permute-start(bf16[128,128]{1,0:T(8,128)(2,1)S(1)} %add_convert_fusion), channel_id=1, source_target_pairs={{0,24},{8,16},{16,8},{24,0},{2,26},{10,18},{18,10},{26,2},{4,28},{... | collective-permute-start | bytes 98312 | tf_op jit(solution)/shard_map/ppermute | solution.py:129
  24.0 1.9 %collective-permute-start.12 = (bf16[128,128]{1,0:T(8,128)(2,1)S(1)}, bf16[128,128]{1,0:T(8,128)(2,1)S(1)}, u32[]{:S(2)}, u32[]{:S(2)}) collective-permute-start(bf16[128,128]{1,0:T(8,128)(2,1)S(1)} %add_convert_fusion), channel_id=1, source_target_pairs={{0,6},{2,4},{4,2},{6,0},{8,14},{10,12},{12,10},{14,8},{16,22},{18,... | collective-permute-start | bytes 98312 | tf_op jit(solution)/shard_map/ppermute | solution.py:129
  25.9 0.0 collective-permute-done.10
  25.9 0.0 collective-permute-done.9
  25.9 2.1 %collective-permute-done.8 = bf16[128,128]{1,0:T(8,128)(2,1)S(1)} collective-permute-done((bf16[128,128]{1,0:T(8,128)(2,1)S(1)}, bf16[128,128]{1,0:T(8,128)(2,1)S(1)}, u32[]{:S(2)}, u32[]{:S(2)}) %collective-permute-start.8) | collective-permute-done | bytes 32800 | tf_op jit(solution)/shard_map/ppermute | solution.py:129
  28.0 1.9 %collective-permute-start.13 = (bf16[384,128]{1,0:T(8,128)(2,1)S(1)}, bf16[384,128]{1,0:T(8,128)(2,1)S(1)}, u32[]{:S(2)}, u32[]{:S(2)}) collective-permute-start(bf16[384,128]{1,0:T(8,128)(2,1)S(1)} %pad_maximum_fusion.2), channel_id=1, source_target_pairs={{0,6},{2,4},{4,2},{6,0},{8,14},{10,12},{12,10},{14,8},{16,22},{18,... | collective-permute-start | bytes 294920 | tf_op jit(solution)/shard_map/ppermute | solution.py:129
  30.0 0.0 copy-start
  30.0 1.2 %collective-permute-start.11 = (bf16[256,128]{1,0:T(8,128)(2,1)S(1)}, bf16[256,128]{1,0:T(8,128)(2,1)S(1)}, u32[]{:S(2)}, u32[]{:S(2)}) collective-permute-start(bf16[256,128]{1,0:T(8,128)(2,1)S(1)} %pad_maximum_fusion.3), channel_id=1, source_target_pairs={{0,4},{2,6},{4,0},{6,2},{8,12},{10,14},{12,8},{14,10},{16,20},{18,... | collective-permute-start | bytes 196616 | tf_op jit(solution)/shard_map/ppermute | solution.py:129
  31.1 0.6 %collective-permute-start.14 = (bf16[512,128]{1,0:T(8,128)(2,1)S(1)}, bf16[512,128]{1,0:T(8,128)(2,1)S(1)}, u32[]{:S(2)}, u32[]{:S(2)}) collective-permute-start(bf16[512,128]{1,0:T(8,128)(2,1)S(1)} %pad_maximum_fusion.refs_0_), channel_id=1, source_target_pairs={{0,2},{2,0},{4,6},{6,4},{8,10},{10,8},{12,14},{14,12},{16,18},{18,... | collective-permute-start | bytes 393224 | tf_op jit(solution)/shard_map/ppermute | solution.py:129
  31.7 0.9 %collective-permute-start.15 = (bf16[256,128]{1,0:T(8,128)(2,1)S(1)}, bf16[256,128]{1,0:T(8,128)(2,1)S(1)}, u32[]{:S(2)}, u32[]{:S(2)}) collective-permute-start(bf16[256,128]{1,0:T(8,128)(2,1)S(1)} %pad_maximum_fusion.4), channel_id=1, source_target_pairs={{0,4},{2,6},{4,0},{6,2},{8,12},{10,14},{12,8},{14,10},{16,20},{18,... | collective-permute-start | bytes 196616 | tf_op jit(solution)/shard_map/ppermute | solution.py:129
  32.7 0.0 collective-permute-done.12.refs_2_
  32.7 2.2 %collective-permute-done.11.refs_1_ = bf16[256,128]{1,0:T(8,128)(2,1)S(1)} collective-permute-done((bf16[256,128]{1,0:T(8,128)(2,1)S(1)}, bf16[256,128]{1,0:T(8,128)(2,1)S(1)}, u32[]{:S(2)}, u32[]{:S(2)}) %collective-permute-start.11) | collective-permute-done | bytes 65568 | tf_op jit(solution)/shard_map/ppermute | solution.py:129
  34.8 0.0 copy-done
  34.8 1.3 %shard_map.69.refs_0_ = f32[172,256]{1,0:T(8,128)S(1)} custom-call(bf16[256,2048]{1,0:T(8,128)(2,1)S(1)} %get-tuple-element.10.high_ref, bf16[256,2048]{1,0:T(8,128)(2,1)S(1)} %get-tuple-element.11.low_ref, bf16[512,128]{1,0:T(8,128)(2,1)S(1)} %get-tuple-element.12.w_in_t_ref, bf16[172,512]{1,0:T(8,128)(2,1)S(1)} %bitcast.23, ...), custom_call_target="tpu_custom_call" | custom-call | flops 247463936 | bytes 1048576 | tf_op jit(solution)/shard_map/pallas_call | solution.py:194
  36.1 0.0 collective-permute-done.13.refs_1_
  36.1 0.7 %shard_map.70.refs_0_ = f32[172,256]{1,0:T(8,128)S(1)} custom-call(bf16[256,2048]{1,0:T(8,128)(2,1)S(1)} %get-tuple-element.10.high_ref, bf16[256,2048]{1,0:T(8,128)(2,1)S(1)} %get-tuple-element.11.low_ref, bf16[512,128]{1,0:T(8,128)(2,1)S(1)} %get-tuple-element.12.w_in_t_ref, bf16[172,512]{1,0:T(8,128)(2,1)S(1)} %bitcast.24, ...), custom_call_target="tpu_custom_call" | custom-call | flops 247463936 | bytes 1048576 | tf_op jit(solution)/shard_map/pallas_call | solution.py:194
  36.8 0.0 collective-permute-done.15.refs_2_
  36.9 0.0 collective-permute-done.14.refs_1_
  36.9 1.1 %shard_map.71 = (f32[172,128]{1,0:T(8,128)S(1)}, f32[172,128]{1,0:T(8,128)S(1)}) custom-call(bf16[256,2048]{1,0:T(8,128)(2,1)S(1)} %get-tuple-element.10.high_ref, bf16[256,2048]{1,0:T(8,128)(2,1)S(1)} %get-tuple-element.11.low_ref, bf16[512,128]{1,0:T(8,128)(2,1)S(1)} %get-tuple-element.12.w_in_t_ref, bf16[172,512]{1,0:T(8,128)(2,1)S(1)} %bitcast.25, ...), custom_call_target="tpu_custom_call" | custom-call | flops 247463936 | bytes 1048576 | tf_op jit(solution)/shard_map/pallas_call | solution.py:194
  38.0 0.1 collective-permute-start.16
  38.1 1.3 %collective-permute-done.16 = f32[172,128]{1,0:T(8,128)S(1)} collective-permute-done((f32[172,128]{1,0:T(8,128)S(1)}, f32[172,128]{1,0:T(8,128)S(1)}, u32[]{:S(2)}, u32[]{:S(2)}) %collective-permute-start.16) | collective-permute-done | bytes 88096 | tf_op jit(solution)/shard_map/ppermute | solution.py:159
  39.3 0.7 %add_bitcast_fusion = f32[128,172]{0,1:T(8,128)} fusion(f32[172,128]{1,0:T(8,128)S(1)} %get-tuple-element.13, f32[172,128]{1,0:T(8,128)S(1)} %collective-permute-done.16), kind=kLoop, calls=%fused_computation.3 | loop fusion | flops 22016 | bytes 264192 | tf_op jit(solution)/shard_map/transpose | solution.py:288
  (10 shorter events, 0.1 us)
Async XLA Ops:
  0.0 8.8 %collective-permute-start = (bf16[128,128]{1,0:T(8,128)(2,1)}, bf16[128,128]{1,0:T(8,128)(2,1)S(1)}, u32[]{:S(2)}, u32[]{:S(2)}) collective-permute-start(bf16[128,128]{1,0:T(8,128)(2,1)} %param.6), channel_id=1, source_target_pairs={{0,24},{8,16},{16,8},{24,0},{2,26},{10,18},{18,10},{26,2},{4,28},{... | collective-permute-start | bytes 98312 | tf_op jit(solution)/shard_map/ppermute | solution.py:129
  5.1 5.0 %collective-permute-start.1 = (bf16[128,128]{1,0:T(8,128)(2,1)}, bf16[128,128]{1,0:T(8,128)(2,1)S(1)}, u32[]{:S(2)}, u32[]{:S(2)}) collective-permute-start(bf16[128,128]{1,0:T(8,128)(2,1)} %param.6), channel_id=1, source_target_pairs={{0,16},{8,24},{16,0},{24,8},{2,18},{10,26},{18,2},{26,10},{4,20},{... | collective-permute-start | bytes 98312 | tf_op jit(solution)/shard_map/ppermute | solution.py:129
  5.1 5.0 %collective-permute-start.2 = (bf16[128,128]{1,0:T(8,128)(2,1)}, bf16[128,128]{1,0:T(8,128)(2,1)S(1)}, u32[]{:S(2)}, u32[]{:S(2)}) collective-permute-start(bf16[128,128]{1,0:T(8,128)(2,1)} %param.6), channel_id=1, source_target_pairs={{0,8},{8,0},{16,24},{24,16},{2,10},{10,2},{18,26},{26,18},{4,12},{... | collective-permute-start | bytes 98312 | tf_op jit(solution)/shard_map/ppermute | solution.py:129
  5.6 10.2 %collective-permute-start.3 = (bf16[128,128]{1,0:T(8,128)(2,1)}, bf16[128,128]{1,0:T(8,128)(2,1)S(1)}, u32[]{:S(2)}, u32[]{:S(2)}) collective-permute-start(bf16[128,128]{1,0:T(8,128)(2,1)} %param.6), channel_id=1, source_target_pairs={{0,4},{2,6},{4,0},{6,2},{8,12},{10,14},{12,8},{14,10},{16,20},{18,... | collective-permute-start | bytes 98312 | tf_op jit(solution)/shard_map/ppermute | solution.py:129
  10.1 3.8 %copy-start.2 = (bf16[128,512]{1,0:T(8,128)(2,1)S(1)}, bf16[128,512]{1,0:T(8,128)(2,1)}, u32[]{:S(2)}) copy-start(bf16[128,512]{1,0:T(8,128)(2,1)} %w_in_ref.1) | copy-start | bytes 393220
  10.1 6.2 %collective-permute-start.4 = (bf16[512,128]{1,0:T(8,128)(2,1)S(1)}, bf16[512,128]{1,0:T(8,128)(2,1)S(1)}, u32[]{:S(2)}, u32[]{:S(2)}) collective-permute-start(bf16[512,128]{1,0:T(8,128)(2,1)S(1)} %constant_dynamic-update-slice_fusion.refs_0_), channel_id=1, source_target_pairs={{0,6},{2,4},{4,2},{6,0},{8,14},{10,12},{12,10},{14,8},{16,22},{18,... | collective-permute-start | bytes 393224 | tf_op jit(solution)/shard_map/ppermute | solution.py:129
  12.7 5.2 %collective-permute-start.5 = (bf16[512,128]{1,0:T(8,128)(2,1)S(1)}, bf16[512,128]{1,0:T(8,128)(2,1)S(1)}, u32[]{:S(2)}, u32[]{:S(2)}) collective-permute-start(bf16[512,128]{1,0:T(8,128)(2,1)S(1)} %constant_dynamic-update-slice_fusion.refs_0_), channel_id=1, source_target_pairs={{0,2},{2,0},{4,6},{6,4},{8,10},{10,8},{12,14},{14,12},{16,18},{18,... | collective-permute-start | bytes 393224 | tf_op jit(solution)/shard_map/ppermute | solution.py:129
  13.2 0.7 %copy-start.3 = (s32[1,1,8]{2,1,0:T(1,128)S(1)}, s32[1,1,8]{2,1,0:T(1,128)}, u32[]{:S(2)}) copy-start(s32[1,1,8]{2,1,0:T(1,128)} %param.7) | copy-start | bytes 100
  13.2 4.7 %collective-permute-start.6 = (bf16[384,128]{1,0:T(8,128)(2,1)S(1)}, bf16[384,128]{1,0:T(8,128)(2,1)S(1)}, u32[]{:S(2)}, u32[]{:S(2)}) collective-permute-start(bf16[384,128]{1,0:T(8,128)(2,1)S(1)} %pad_maximum_fusion.1), channel_id=1, source_target_pairs={{0,4},{2,6},{4,0},{6,2},{8,12},{10,14},{12,8},{14,10},{16,20},{18,... | collective-permute-start | bytes 294920 | tf_op jit(solution)/shard_map/ppermute | solution.py:129
  13.9 1.0 %copy-start.1 = (f32[1,1,8,128,128]{4,3,2,1,0:T(8,128)S(1)}, f32[1,1,8,128,128]{4,3,2,1,0:T(8,128)}, u32[]{:S(2)}) copy-start(f32[1,1,8,128,128]{4,3,2,1,0:T(8,128)} %param.9) | copy-start | bytes 1572868
  18.2 1.3 %collective-permute-start.7 = (f32[128,128]{1,0:T(8,128)S(1)}, f32[128,128]{1,0:T(8,128)S(1)}, u32[]{:S(2)}, u32[]{:S(2)}) collective-permute-start(f32[128,128]{1,0:T(8,128)S(1)} %shard_map.68), channel_id=1, source_target_pairs={{0,1},{1,0},{2,3},{3,2},{4,5},{5,4},{6,7},{7,6},{8,9},{9,8},{10,11... | collective-permute-start | bytes 196616 | tf_op jit(solution)/shard_map/ppermute | solution.py:159
  19.5 6.4 %collective-permute-start.10 = (bf16[128,128]{1,0:T(8,128)(2,1)S(1)}, bf16[128,128]{1,0:T(8,128)(2,1)S(1)}, u32[]{:S(2)}, u32[]{:S(2)}) collective-permute-start(bf16[128,128]{1,0:T(8,128)(2,1)S(1)} %add_convert_fusion), channel_id=1, source_target_pairs={{0,8},{8,0},{16,24},{24,16},{2,10},{10,2},{18,26},{26,18},{4,12},{... | collective-permute-start | bytes 98312 | tf_op jit(solution)/shard_map/ppermute | solution.py:129
  19.7 6.2 %collective-permute-start.9 = (bf16[128,128]{1,0:T(8,128)(2,1)S(1)}, bf16[128,128]{1,0:T(8,128)(2,1)S(1)}, u32[]{:S(2)}, u32[]{:S(2)}) collective-permute-start(bf16[128,128]{1,0:T(8,128)(2,1)S(1)} %add_convert_fusion), channel_id=1, source_target_pairs={{0,16},{8,24},{16,0},{24,8},{2,18},{10,26},{18,2},{26,10},{4,20},{... | collective-permute-start | bytes 98312 | tf_op jit(solution)/shard_map/ppermute | solution.py:129
  22.3 5.7 %collective-permute-start.8 = (bf16[128,128]{1,0:T(8,128)(2,1)S(1)}, bf16[128,128]{1,0:T(8,128)(2,1)S(1)}, u32[]{:S(2)}, u32[]{:S(2)}) collective-permute-start(bf16[128,128]{1,0:T(8,128)(2,1)S(1)} %add_convert_fusion), channel_id=1, source_target_pairs={{0,24},{8,16},{16,8},{24,0},{2,26},{10,18},{18,10},{26,2},{4,28},{... | collective-permute-start | bytes 98312 | tf_op jit(solution)/shard_map/ppermute | solution.py:129
  24.0 8.7 %collective-permute-start.12 = (bf16[128,128]{1,0:T(8,128)(2,1)S(1)}, bf16[128,128]{1,0:T(8,128)(2,1)S(1)}, u32[]{:S(2)}, u32[]{:S(2)}) collective-permute-start(bf16[128,128]{1,0:T(8,128)(2,1)S(1)} %add_convert_fusion), channel_id=1, source_target_pairs={{0,6},{2,4},{4,2},{6,0},{8,14},{10,12},{12,10},{14,8},{16,22},{18,... | collective-permute-start | bytes 98312 | tf_op jit(solution)/shard_map/ppermute | solution.py:129
  28.0 8.1 %collective-permute-start.13 = (bf16[384,128]{1,0:T(8,128)(2,1)S(1)}, bf16[384,128]{1,0:T(8,128)(2,1)S(1)}, u32[]{:S(2)}, u32[]{:S(2)}) collective-permute-start(bf16[384,128]{1,0:T(8,128)(2,1)S(1)} %pad_maximum_fusion.2), channel_id=1, source_target_pairs={{0,6},{2,4},{4,2},{6,0},{8,14},{10,12},{12,10},{14,8},{16,22},{18,... | collective-permute-start | bytes 294920 | tf_op jit(solution)/shard_map/ppermute | solution.py:129
  30.0 4.9 %copy-start = (bf16[512,172]{0,1:T(8,128)(2,1)S(1)}, bf16[512,172]{0,1:T(8,128)(2,1)}, u32[]{:S(2)}) copy-start(bf16[512,172]{0,1:T(8,128)(2,1)} %param.11) | copy-start | bytes 528388
  30.0 4.9 %collective-permute-start.11 = (bf16[256,128]{1,0:T(8,128)(2,1)S(1)}, bf16[256,128]{1,0:T(8,128)(2,1)S(1)}, u32[]{:S(2)}, u32[]{:S(2)}) collective-permute-start(bf16[256,128]{1,0:T(8,128)(2,1)S(1)} %pad_maximum_fusion.3), channel_id=1, source_target_pairs={{0,4},{2,6},{4,0},{6,2},{8,12},{10,14},{12,8},{14,10},{16,20},{18,... | collective-permute-start | bytes 196616 | tf_op jit(solution)/shard_map/ppermute | solution.py:129
  31.1 5.7 %collective-permute-start.14 = (bf16[512,128]{1,0:T(8,128)(2,1)S(1)}, bf16[512,128]{1,0:T(8,128)(2,1)S(1)}, u32[]{:S(2)}, u32[]{:S(2)}) collective-permute-start(bf16[512,128]{1,0:T(8,128)(2,1)S(1)} %pad_maximum_fusion.refs_0_), channel_id=1, source_target_pairs={{0,2},{2,0},{4,6},{6,4},{8,10},{10,8},{12,14},{14,12},{16,18},{18,... | collective-permute-start | bytes 393224 | tf_op jit(solution)/shard_map/ppermute | solution.py:129
  31.7 5.1 %collective-permute-start.15 = (bf16[256,128]{1,0:T(8,128)(2,1)S(1)}, bf16[256,128]{1,0:T(8,128)(2,1)S(1)}, u32[]{:S(2)}, u32[]{:S(2)}) collective-permute-start(bf16[256,128]{1,0:T(8,128)(2,1)S(1)} %pad_maximum_fusion.4), channel_id=1, source_target_pairs={{0,4},{2,6},{4,0},{6,2},{8,12},{10,14},{12,8},{14,10},{16,20},{18,... | collective-permute-start | bytes 196616 | tf_op jit(solution)/shard_map/ppermute | solution.py:129
  38.0 1.4 %collective-permute-start.16 = (f32[172,128]{1,0:T(8,128)S(1)}, f32[172,128]{1,0:T(8,128)S(1)}, u32[]{:S(2)}, u32[]{:S(2)}) collective-permute-start(f32[172,128]{1,0:T(8,128)S(1)} %get-tuple-element.14), channel_id=1, source_target_pairs={{0,1},{1,0},{2,3},{3,2},{4,5},{5,4},{6,7},{7,6},{8,9},{9,8},{10,11... | collective-permute-start | bytes 264200 | tf_op jit(solution)/shard_map/ppermute | solution.py:159
where the time goes:
time: 40.2 us; the launch traced here: 40 us
  starting transfers between devices  22.1 us (55%)
  waiting for transfers between devices  9.19 us (23%)
  Pallas kernels  5.17 us (13%)
  local copies, waits for them, and re-layouts  1.95 us (5%)
  between operations  0.84 us (2%)
  other arithmetic  0.72 us (2%)
    ppermute x15, starting transfers between devices, hop(): return lax.ppermute(value, 'tgt', pairs)  22 us
    ppermute x15, waiting for transfers between devices, hop(): return lax.ppermute(value, 'tgt', pairs)  6.96 us
    pallas_call x8, Pallas kernels, call(): pl.pallas_call(kernel, out_shape=outs, in_specs=[SMEM] * n_small + [VMEM]...  5.17 us
    ppermute x2, waiting for transfers between devices, to_owner(): moved.append(lax.ppermute(part, 'src', pairs))  2.23 us
    unnamed x11, local copies, waits for them, and re-layouts  1.93 us
  transfers between devices with their start and end apart: 17, of which 7 were waited for; matrix products, arithmetic and copies ran while one was open for 2% of the time, Pallas kernels for 9%

commit v1 on v0

--- a/solution.py
+++ b/solution.py
@@ -12,7 +12,7 @@
 SMEM = pl.BlockSpec(memory_space=pltpu.SMEM)
 GRANT = pltpu.CompilerParams(vmem_limit_bytes=24 << 20)
 DIRECT = 4
-CFG = {"p": ((3, 2, 1), {2: 1}, (3, 1, 2)), "s": ((3, 2, 1), {3: 1, 2: 2}, (3, 1, 2))}
+CFG = {"p": ((3, 2, 1), {2: 1}, (3, 1, 2)), "s": ((3, 1, 2), {3: 1, 2: 2}, (3, 1, 2))}
 EARLY, MIDDLE, LATE = ((0, True), (1, False), (2, False), (3, False)), ((3, True),), ((1, True), (2, True))
 
 
@@ -56,10 +56,6 @@
     return lax.dot_general(left, right, (((1,), (1,)), ((), ())), preferred_element_type=jnp.float32)
 
 
-def times_rows(message, high_ref, low_ref, rows, columns):
-    return times_transposed(message, high_ref[rows, columns]) + times_transposed(message, low_ref[rows, columns])
-
-
 def transform(agg, w_in_t_ref, w_out_t_ref):
     hidden = jnp.maximum(times_transposed(w_in_t_ref[...], agg), 0.0).astype(jnp.bfloat16)
     return jnp.dot(w_out_t_ref[...], hidden, preferred_element_type=jnp.float32).astype(jnp.bfloat16)
@@ -73,13 +69,13 @@
         out[...] = rows_times(high_ref, low_ref, slice(d * own, (d + 1) * own), slice(None), picked)
 
 
-def second_kernel(count, tile, spot_ref, high_ref, low_ref, w_in_t_ref, w_out_t_ref, *refs):
+def second_kernel(count, tile, spot_ref, high_ref, w_in_t_ref, w_out_t_ref, *refs):
     pieces, outs, (joined_ref, picked_ref) = refs[:count], refs[count:-2], refs[-2:]
     pick(spot_ref, pieces, joined_ref, picked_ref, tile)
     message = transform(picked_ref[...], w_in_t_ref, w_out_t_ref)
     own = outs[0].shape[1]
     for d, out in enumerate(outs):
-        out[...] = times_rows(message, high_ref, low_ref, slice(d * own, (d + 1) * own), slice(None))
+        out[...] = times_transposed(message, high_ref[d * own : (d + 1) * own, :])
 
 
 def place_dense_kernel(code_ref, spot_ref, tiles_ref, w_in_ref, high_ref, low_ref, w_in_t_ref):
@@ -109,15 +105,15 @@
     out_ref[...] = total
 
 
-def second_dense_kernel(spans, own, summed, high_ref, low_ref, w_in_t_ref, w_out_t_ref, *refs):
+def second_dense_kernel(spans, own, summed, high_ref, w_in_t_ref, w_out_t_ref, *refs):
     count = len(spans)
     before, pieces, outs = refs[:summed], refs[summed : summed + count], refs[summed + count :]
+    total = before[0][...] if summed else None
     message = transform(jnp.concatenate([piece[...] for piece in pieces], 0), w_in_t_ref, w_out_t_ref)
-    total = before[0][...] if summed else None
     base = 0
     for columns in spans:
         size = columns.stop - columns.start
-        term = times_rows(message[:, base : base + size], high_ref, low_ref, slice(None), columns)
+        term = times_transposed(message[:, base : base + size], high_ref[:, columns])
         total = term if total is None else total + term
         base += size
     for d, out in enumerate(outs):
@@ -268,9 +264,9 @@
                 kernel,
                 [out_part] * n_src if last else [pltpu.VMEM((classes, all_rows), jnp.float32)],
                 0,
-                (high, low, w_in_t, w_out_t, *before, *held),
+                (high, w_in_t, w_out_t, *before, *held),
                 (),
-                own * outer * (weights + 4 * all_rows * classes),
+                own * outer * (weights + 2 * all_rows * classes),
             )
 
         early = second(EARLY, (), False)
@@ -281,9 +277,9 @@
             functools.partial(second_kernel, len(pieces), tile),
             [out_part] * n_src,
             1,
-            (spot, high, low, w_in_t, w_out_t, *pieces),
+            (spot, high, w_in_t, w_out_t, *pieces),
             scratch,
-            depth * (weights + 4 * all_rows * classes),
+            depth * (weights + 2 * all_rows * classes),
         )
     return sum(to_owner(others, n_src), mine).T
 

time: 40.2 us -> 37.1 us (0.923)
  waiting for transfers between devices: 9.19 us -> 6.61 us
  Pallas kernels: 5.17 us -> 4.47 us
    ppermute x15, waiting for transfers between devices: 6.96 us -> 4.38 us  [hop(): return lax.ppermute(value, 'tgt', pairs)]
    pallas_call x8, Pallas kernels: 5.17 us -> 4.47 us  [call(): pl.pallas_call(kernel, out_shape=outs, in_specs=[SMEM] * n_small + [VMEM]...]
  transfers between devices with their start and end apart: 17 -> 17, of which waited for: 7 -> 8; matrix products, arithmetic and copies ran while one was open for 2% -> 2% of each run, Pallas kernels for 9% -> 9%
where the time goes in v1:
time: 37.1 us; the launch traced here: 36.8 us
  starting transfers between devices  22.2 us (60%)
  waiting for transfers between devices  6.61 us (18%)
  Pallas kernels  4.47 us (12%)
  local copies, waits for them, and re-layouts  1.95 us (5%)
  between operations  0.82 us (2%)
  other arithmetic  0.72 us (2%)
    ppermute x15, starting transfers between devices, hop(): return lax.ppermute(value, 'tgt', pairs)  22.1 us
    pallas_call x8, Pallas kernels, call(): pl.pallas_call(kernel, out_shape=outs, in_specs=[SMEM] * n_small + [VMEM]...  4.47 us
    ppermute x15, waiting for transfers between devices, hop(): return lax.ppermute(value, 'tgt', pairs)  4.38 us
    ppermute x2, waiting for transfers between devices, to_owner(): moved.append(lax.ppermute(part, 'src', pairs))  2.23 us
    unnamed x11, local copies, waits for them, and re-layouts  1.94 us
  transfers between devices with their start and end apart: 17, of which 8 were waited for; matrix products, arithmetic and copies ran while one was open for 2% of the time, Pallas kernels for 9%

profile of v1, /device:TPU:0, one launch (start us, length us, event | category | flops | bytes accessed | tf_op | source)
XLA Modules:
  0.0 36.8 jit_solution(3285500641075789981)
XLA Ops:
  0.0 5.1 %collective-permute-start = (bf16[128,128]{1,0:T(8,128)(2,1)}, bf16[128,128]{1,0:T(8,128)(2,1)S(1)}, u32[]{:S(2)}, u32[]{:S(2)}) collective-permute-start(bf16[128,128]{1,0:T(8,128)(2,1)} %param.6), channel_id=1, source_target_pairs={{0,24},{8,16},{16,8},{24,0},{2,26},{10,18},{18,10},{26,2},{4,28},{... | collective-permute-start | bytes 98312 | tf_op jit(solution)/shard_map/ppermute | solution.py:125
  5.1 0.0 collective-permute-start.1
  5.1 0.6 %collective-permute-start.2 = (bf16[128,128]{1,0:T(8,128)(2,1)}, bf16[128,128]{1,0:T(8,128)(2,1)S(1)}, u32[]{:S(2)}, u32[]{:S(2)}) collective-permute-start(bf16[128,128]{1,0:T(8,128)(2,1)} %param.6), channel_id=1, source_target_pairs={{0,8},{8,0},{16,24},{24,16},{2,10},{10,2},{18,26},{26,18},{4,12},{... | collective-permute-start | bytes 98312 | tf_op jit(solution)/shard_map/ppermute | solution.py:125
  5.6 1.7 %collective-permute-start.3 = (bf16[128,128]{1,0:T(8,128)(2,1)}, bf16[128,128]{1,0:T(8,128)(2,1)S(1)}, u32[]{:S(2)}, u32[]{:S(2)}) collective-permute-start(bf16[128,128]{1,0:T(8,128)(2,1)} %param.6), channel_id=1, source_target_pairs={{0,4},{2,6},{4,0},{6,2},{8,12},{10,14},{12,8},{14,10},{16,20},{18,... | collective-permute-start | bytes 98312 | tf_op jit(solution)/shard_map/ppermute | solution.py:125
  7.4 0.8 %constant_dynamic-update-slice_fusion.3 = bf16[512,128]{1,0:T(8,128)(2,1)S(1)} fusion(bf16[128,128]{1,0:T(8,128)(2,1)} %param.6), kind=kLoop, calls=%fused_computation.10 | loop fusion | bytes 65536
  8.8 0.0 collective-permute-done
  8.9 1.2 %collective-permute-done.1 = bf16[128,128]{1,0:T(8,128)(2,1)S(1)} collective-permute-done((bf16[128,128]{1,0:T(8,128)(2,1)}, bf16[128,128]{1,0:T(8,128)(2,1)S(1)}, u32[]{:S(2)}, u32[]{:S(2)}) %collective-permute-start.1) | collective-permute-done | bytes 32800 | tf_op jit(solution)/shard_map/ppermute | solution.py:125
  10.1 0.0 copy-start.2
  10.1 0.0 collective-permute-done.2
  10.1 2.5 %collective-permute-start.4 = (bf16[512,128]{1,0:T(8,128)(2,1)S(1)}, bf16[512,128]{1,0:T(8,128)(2,1)S(1)}, u32[]{:S(2)}, u32[]{:S(2)}) collective-permute-start(bf16[512,128]{1,0:T(8,128)(2,1)S(1)} %constant_dynamic-update-slice_fusion.refs_0_), channel_id=1, source_target_pairs={{0,6},{2,4},{4,2},{6,0},{8,14},{10,12},{12,10},{14,8},{16,22},{18,... | collective-permute-start | bytes 393224 | tf_op jit(solution)/shard_map/ppermute | solution.py:125
  12.7 0.5 %collective-permute-start.5 = (bf16[512,128]{1,0:T(8,128)(2,1)S(1)}, bf16[512,128]{1,0:T(8,128)(2,1)S(1)}, u32[]{:S(2)}, u32[]{:S(2)}) collective-permute-start(bf16[512,128]{1,0:T(8,128)(2,1)S(1)} %constant_dynamic-update-slice_fusion.refs_0_), channel_id=1, source_target_pairs={{0,2},{2,0},{4,6},{6,4},{8,10},{10,8},{12,14},{14,12},{16,18},{18,... | collective-permute-start | bytes 393224 | tf_op jit(solution)/shard_map/ppermute | solution.py:125
  13.2 0.0 copy-start.3
  13.2 0.6 %collective-permute-start.6 = (bf16[384,128]{1,0:T(8,128)(2,1)S(1)}, bf16[384,128]{1,0:T(8,128)(2,1)S(1)}, u32[]{:S(2)}, u32[]{:S(2)}) collective-permute-start(bf16[384,128]{1,0:T(8,128)(2,1)S(1)} %pad_maximum_fusion.1), channel_id=1, source_target_pairs={{0,4},{2,6},{4,0},{6,2},{8,12},{10,14},{12,8},{14,10},{16,20},{18,... | collective-permute-start | bytes 294920 | tf_op jit(solution)/shard_map/ppermute | solution.py:125
  13.8 0.1 copy-done.3
  13.9 0.0 copy-done.2
  13.9 0.0 copy-start.1
  13.9 1.0 %copy-done.1 = f32[1,1,8,128,128]{4,3,2,1,0:T(8,128)S(1)} copy-done((f32[1,1,8,128,128]{4,3,2,1,0:T(8,128)S(1)}, f32[1,1,8,128,128]{4,3,2,1,0:T(8,128)}, u32[]{:S(2)}) %copy-start.1) | copy-done | bytes 524312
  14.9 0.9 %shard_map.64 = (bf16[256,2048]{1,0:T(8,128)(2,1)S(1)}, bf16[256,2048]{1,0:T(8,128)(2,1)S(1)}, bf16[512,128]{1,0:T(8,128)(2,1)S(1)}) custom-call(s32[8]{0:T(128)S(1)} %get-tuple-element.16.code_ref, s32[8]{0:T(128)S(1)} %get-tuple-element.15.spot_ref, f32[8,128,128]{2,1,0:T(8,128)S(1)} %bitcast.26, bf16[128,512]{1,0:T(8,128)(2,1)S(1)} %copy-done.2), custom_call_target="tpu_custom_call" | custom-call | bytes 1048576 | tf_op jit(solution)/shard_map/pallas_call | solution.py:190
  15.9 0.0 collective-permute-done.3.refs_1_
  15.9 0.3 shard_map.65.refs_0_
  16.2 0.1 collective-permute-done.4.refs_1_
  16.3 0.3 shard_map.66.refs_0_
  16.6 1.3 %collective-permute-done.6.refs_2_ = bf16[384,128]{1,0:T(8,128)(2,1)S(1)} collective-permute-done((bf16[384,128]{1,0:T(8,128)(2,1)S(1)}, bf16[384,128]{1,0:T(8,128)(2,1)S(1)}, u32[]{:S(2)}, u32[]{:S(2)}) %collective-permute-start.6) | collective-permute-done | bytes 98336 | tf_op jit(solution)/shard_map/ppermute | solution.py:125
  17.9 0.0 collective-permute-done.5.refs_1_
  17.9 0.3 shard_map.68
  18.2 0.1 collective-permute-start.7
  18.3 0.3 shard_map.67
  18.5 1.0 %collective-permute-done.7 = f32[128,128]{1,0:T(8,128)S(1)} collective-permute-done((f32[128,128]{1,0:T(8,128)S(1)}, f32[128,128]{1,0:T(8,128)S(1)}, u32[]{:S(2)}, u32[]{:S(2)}) %collective-permute-start.7) | collective-permute-done | bytes 65568 | tf_op jit(solution)/shard_map/ppermute | solution.py:155
  19.5 2.2 %collective-permute-start.8 = (bf16[128,128]{1,0:T(8,128)(2,1)S(1)}, bf16[128,128]{1,0:T(8,128)(2,1)S(1)}, u32[]{:S(2)}, u32[]{:S(2)}) collective-permute-start(bf16[128,128]{1,0:T(8,128)(2,1)S(1)} %add_convert_fusion), channel_id=1, source_target_pairs={{0,24},{8,16},{16,8},{24,0},{2,26},{10,18},{18,10},{26,2},{4,28},{... | collective-permute-start | bytes 98312 | tf_op jit(solution)/shard_map/ppermute | solution.py:125
  21.8 0.3 collective-permute-start.10
  22.1 1.9 %collective-permute-start.9 = (bf16[128,128]{1,0:T(8,128)(2,1)S(1)}, bf16[128,128]{1,0:T(8,128)(2,1)S(1)}, u32[]{:S(2)}, u32[]{:S(2)}) collective-permute-start(bf16[128,128]{1,0:T(8,128)(2,1)S(1)} %add_convert_fusion), channel_id=1, source_target_pairs={{0,16},{8,24},{16,0},{24,8},{2,18},{10,26},{18,2},{26,10},{4,20},{... | collective-permute-start | bytes 98312 | tf_op jit(solution)/shard_map/ppermute | solution.py:125
  24.0 1.9 %collective-permute-start.12 = (bf16[128,128]{1,0:T(8,128)(2,1)S(1)}, bf16[128,128]{1,0:T(8,128)(2,1)S(1)}, u32[]{:S(2)}, u32[]{:S(2)}) collective-permute-start(bf16[128,128]{1,0:T(8,128)(2,1)S(1)} %add_convert_fusion), channel_id=1, source_target_pairs={{0,6},{2,4},{4,2},{6,0},{8,14},{10,12},{12,10},{14,8},{16,22},{18,... | collective-permute-start | bytes 98312 | tf_op jit(solution)/shard_map/ppermute | solution.py:125
  25.9 0.0 collective-permute-done.8
  25.9 1.1 %collective-permute-start.11 = (bf16[256,128]{1,0:T(8,128)(2,1)S(1)}, bf16[256,128]{1,0:T(8,128)(2,1)S(1)}, u32[]{:S(2)}, u32[]{:S(2)}) collective-permute-start(bf16[256,128]{1,0:T(8,128)(2,1)S(1)} %pad_maximum_fusion.3), channel_id=1, source_target_pairs={{0,4},{2,6},{4,0},{6,2},{8,12},{10,14},{12,8},{14,10},{16,20},{18,... | collective-permute-start | bytes 196616 | tf_op jit(solution)/shard_map/ppermute | solution.py:125
  27.0 0.0 collective-permute-done.10
  27.0 0.0 collective-permute-done.9
  27.0 0.0 copy-start
  27.0 1.9 %collective-permute-start.13 = (bf16[384,128]{1,0:T(8,128)(2,1)S(1)}, bf16[384,128]{1,0:T(8,128)(2,1)S(1)}, u32[]{:S(2)}, u32[]{:S(2)}) collective-permute-start(bf16[384,128]{1,0:T(8,128)(2,1)S(1)} %pad_maximum_fusion.2), channel_id=1, source_target_pairs={{0,6},{2,4},{4,2},{6,0},{8,14},{10,12},{12,10},{14,8},{16,22},{18,... | collective-permute-start | bytes 294920 | tf_op jit(solution)/shard_map/ppermute | solution.py:125
  28.9 0.7 %collective-permute-start.14 = (bf16[512,128]{1,0:T(8,128)(2,1)S(1)}, bf16[512,128]{1,0:T(8,128)(2,1)S(1)}, u32[]{:S(2)}, u32[]{:S(2)}) collective-permute-start(bf16[512,128]{1,0:T(8,128)(2,1)S(1)} %pad_maximum_fusion.refs_0_), channel_id=1, source_target_pairs={{0,2},{2,0},{4,6},{6,4},{8,10},{10,8},{12,14},{14,12},{16,18},{18,... | collective-permute-start | bytes 393224 | tf_op jit(solution)/shard_map/ppermute | solution.py:125
  29.6 1.0 %collective-permute-start.15 = (bf16[256,128]{1,0:T(8,128)(2,1)S(1)}, bf16[256,128]{1,0:T(8,128)(2,1)S(1)}, u32[]{:S(2)}, u32[]{:S(2)}) collective-permute-start(bf16[256,128]{1,0:T(8,128)(2,1)S(1)} %pad_maximum_fusion.4), channel_id=1, source_target_pairs={{0,4},{2,6},{4,0},{6,2},{8,12},{10,14},{12,8},{14,10},{16,20},{18,... | collective-permute-start | bytes 196616 | tf_op jit(solution)/shard_map/ppermute | solution.py:125
  30.7 0.0 collective-permute-done.12.refs_2_
  30.7 1.2 %collective-permute-done.11.refs_1_ = bf16[256,128]{1,0:T(8,128)(2,1)S(1)} collective-permute-done((bf16[256,128]{1,0:T(8,128)(2,1)S(1)}, bf16[256,128]{1,0:T(8,128)(2,1)S(1)}, u32[]{:S(2)}, u32[]{:S(2)}) %collective-permute-start.11) | collective-permute-done | bytes 65568 | tf_op jit(solution)/shard_map/ppermute | solution.py:125
  31.9 0.0 copy-done
  31.9 1.0 %shard_map.69.refs_0_ = f32[172,256]{1,0:T(8,128)S(1)} custom-call(bf16[256,2048]{1,0:T(8,128)(2,1)S(1)} %get-tuple-element.10.high_ref, bf16[512,128]{1,0:T(8,128)(2,1)S(1)} %get-tuple-element.11.w_in_t_ref, bf16[172,512]{1,0:T(8,128)(2,1)S(1)} %bitcast.23, bf16[512,128]{1,0:T(8,128)(2,1)S(1)} %pad_maximum_fusion.refs_0_, ...), custom_call_target="tpu_custom_call" | custom-call | flops 202375168 | bytes 1048576 | tf_op jit(solution)/shard_map/pallas_call | solution.py:190
  32.8 0.0 collective-permute-done.13.refs_1_
  32.9 0.6 %shard_map.70.refs_0_ = f32[172,256]{1,0:T(8,128)S(1)} custom-call(bf16[256,2048]{1,0:T(8,128)(2,1)S(1)} %get-tuple-element.10.high_ref, bf16[512,128]{1,0:T(8,128)(2,1)S(1)} %get-tuple-element.11.w_in_t_ref, bf16[172,512]{1,0:T(8,128)(2,1)S(1)} %bitcast.24, f32[172,256]{1,0:T(8,128)S(1)} %shard_map.69.refs_0_, ...), custom_call_target="tpu_custom_call" | custom-call | flops 202375168 | bytes 1048576 | tf_op jit(solution)/shard_map/pallas_call | solution.py:190
  33.5 0.4 %collective-permute-done.15.refs_2_ = bf16[256,128]{1,0:T(8,128)(2,1)S(1)} collective-permute-done((bf16[256,128]{1,0:T(8,128)(2,1)S(1)}, bf16[256,128]{1,0:T(8,128)(2,1)S(1)}, u32[]{:S(2)}, u32[]{:S(2)}) %collective-permute-start.15) | collective-permute-done | bytes 65568 | tf_op jit(solution)/shard_map/ppermute | solution.py:125
  33.9 0.1 collective-permute-done.14.refs_1_
  34.0 0.8 %shard_map.71 = (f32[172,128]{1,0:T(8,128)S(1)}, f32[172,128]{1,0:T(8,128)S(1)}) custom-call(bf16[256,2048]{1,0:T(8,128)(2,1)S(1)} %get-tuple-element.10.high_ref, bf16[512,128]{1,0:T(8,128)(2,1)S(1)} %get-tuple-element.11.w_in_t_ref, bf16[172,512]{1,0:T(8,128)(2,1)S(1)} %bitcast.25, f32[172,256]{1,0:T(8,128)S(1)} %shard_map.70.refs_0_, ...), custom_call_target="tpu_custom_call" | custom-call | flops 202375168 | bytes 1048576 | tf_op jit(solution)/shard_map/pallas_call | solution.py:190
  34.8 0.1 collective-permute-start.16
  34.9 1.3 %collective-permute-done.16 = f32[172,128]{1,0:T(8,128)S(1)} collective-permute-done((f32[172,128]{1,0:T(8,128)S(1)}, f32[172,128]{1,0:T(8,128)S(1)}, u32[]{:S(2)}, u32[]{:S(2)}) %collective-permute-start.16) | collective-permute-done | bytes 88096 | tf_op jit(solution)/shard_map/ppermute | solution.py:155
  36.2 0.7 %add_bitcast_fusion = f32[128,172]{0,1:T(8,128)} fusion(f32[172,128]{1,0:T(8,128)S(1)} %get-tuple-element.13, f32[172,128]{1,0:T(8,128)S(1)} %collective-permute-done.16), kind=kLoop, calls=%fused_computation.3 | loop fusion | flops 22016 | bytes 264192 | tf_op jit(solution)/shard_map/transpose | solution.py:284
  (10 shorter events, 0.1 us)
Async XLA Ops:
  0.0 8.8 %collective-permute-start = (bf16[128,128]{1,0:T(8,128)(2,1)}, bf16[128,128]{1,0:T(8,128)(2,1)S(1)}, u32[]{:S(2)}, u32[]{:S(2)}) collective-permute-start(bf16[128,128]{1,0:T(8,128)(2,1)} %param.6), channel_id=1, source_target_pairs={{0,24},{8,16},{16,8},{24,0},{2,26},{10,18},{18,10},{26,2},{4,28},{... | collective-permute-start | bytes 98312 | tf_op jit(solution)/shard_map/ppermute | solution.py:125
  5.1 5.0 %collective-permute-start.1 = (bf16[128,128]{1,0:T(8,128)(2,1)}, bf16[128,128]{1,0:T(8,128)(2,1)S(1)}, u32[]{:S(2)}, u32[]{:S(2)}) collective-permute-start(bf16[128,128]{1,0:T(8,128)(2,1)} %param.6), channel_id=1, source_target_pairs={{0,16},{8,24},{16,0},{24,8},{2,18},{10,26},{18,2},{26,10},{4,20},{... | collective-permute-start | bytes 98312 | tf_op jit(solution)/shard_map/ppermute | solution.py:125
  5.1 5.0 %collective-permute-start.2 = (bf16[128,128]{1,0:T(8,128)(2,1)}, bf16[128,128]{1,0:T(8,128)(2,1)S(1)}, u32[]{:S(2)}, u32[]{:S(2)}) collective-permute-start(bf16[128,128]{1,0:T(8,128)(2,1)} %param.6), channel_id=1, source_target_pairs={{0,8},{8,0},{16,24},{24,16},{2,10},{10,2},{18,26},{26,18},{4,12},{... | collective-permute-start | bytes 98312 | tf_op jit(solution)/shard_map/ppermute | solution.py:125
  5.6 10.2 %collective-permute-start.3 = (bf16[128,128]{1,0:T(8,128)(2,1)}, bf16[128,128]{1,0:T(8,128)(2,1)S(1)}, u32[]{:S(2)}, u32[]{:S(2)}) collective-permute-start(bf16[128,128]{1,0:T(8,128)(2,1)} %param.6), channel_id=1, source_target_pairs={{0,4},{2,6},{4,0},{6,2},{8,12},{10,14},{12,8},{14,10},{16,20},{18,... | collective-permute-start | bytes 98312 | tf_op jit(solution)/shard_map/ppermute | solution.py:125
  10.1 3.8 %copy-start.2 = (bf16[128,512]{1,0:T(8,128)(2,1)S(1)}, bf16[128,512]{1,0:T(8,128)(2,1)}, u32[]{:S(2)}) copy-start(bf16[128,512]{1,0:T(8,128)(2,1)} %w_in_ref.1) | copy-start | bytes 393220
  10.1 6.2 %collective-permute-start.4 = (bf16[512,128]{1,0:T(8,128)(2,1)S(1)}, bf16[512,128]{1,0:T(8,128)(2,1)S(1)}, u32[]{:S(2)}, u32[]{:S(2)}) collective-permute-start(bf16[512,128]{1,0:T(8,128)(2,1)S(1)} %constant_dynamic-update-slice_fusion.refs_0_), channel_id=1, source_target_pairs={{0,6},{2,4},{4,2},{6,0},{8,14},{10,12},{12,10},{14,8},{16,22},{18,... | collective-permute-start | bytes 393224 | tf_op jit(solution)/shard_map/ppermute | solution.py:125
  12.7 5.2 %collective-permute-start.5 = (bf16[512,128]{1,0:T(8,128)(2,1)S(1)}, bf16[512,128]{1,0:T(8,128)(2,1)S(1)}, u32[]{:S(2)}, u32[]{:S(2)}) collective-permute-start(bf16[512,128]{1,0:T(8,128)(2,1)S(1)} %constant_dynamic-update-slice_fusion.refs_0_), channel_id=1, source_target_pairs={{0,2},{2,0},{4,6},{6,4},{8,10},{10,8},{12,14},{14,12},{16,18},{18,... | collective-permute-start | bytes 393224 | tf_op jit(solution)/shard_map/ppermute | solution.py:125
  13.2 0.7 %copy-start.3 = (s32[1,1,8]{2,1,0:T(1,128)S(1)}, s32[1,1,8]{2,1,0:T(1,128)}, u32[]{:S(2)}) copy-start(s32[1,1,8]{2,1,0:T(1,128)} %param.7) | copy-start | bytes 100
  13.2 4.7 %collective-permute-start.6 = (bf16[384,128]{1,0:T(8,128)(2,1)S(1)}, bf16[384,128]{1,0:T(8,128)(2,1)S(1)}, u32[]{:S(2)}, u32[]{:S(2)}) collective-permute-start(bf16[384,128]{1,0:T(8,128)(2,1)S(1)} %pad_maximum_fusion.1), channel_id=1, source_target_pairs={{0,4},{2,6},{4,0},{6,2},{8,12},{10,14},{12,8},{14,10},{16,20},{18,... | collective-permute-start | bytes 294920 | tf_op jit(solution)/shard_map/ppermute | solution.py:125
  13.9 1.0 %copy-start.1 = (f32[1,1,8,128,128]{4,3,2,1,0:T(8,128)S(1)}, f32[1,1,8,128,128]{4,3,2,1,0:T(8,128)}, u32[]{:S(2)}) copy-start(f32[1,1,8,128,128]{4,3,2,1,0:T(8,128)} %param.9) | copy-start | bytes 1572868
  18.2 1.3 %collective-permute-start.7 = (f32[128,128]{1,0:T(8,128)S(1)}, f32[128,128]{1,0:T(8,128)S(1)}, u32[]{:S(2)}, u32[]{:S(2)}) collective-permute-start(f32[128,128]{1,0:T(8,128)S(1)} %shard_map.68), channel_id=1, source_target_pairs={{0,1},{1,0},{2,3},{3,2},{4,5},{5,4},{6,7},{7,6},{8,9},{9,8},{10,11... | collective-permute-start | bytes 196616 | tf_op jit(solution)/shard_map/ppermute | solution.py:155
  19.5 6.4 %collective-permute-start.8 = (bf16[128,128]{1,0:T(8,128)(2,1)S(1)}, bf16[128,128]{1,0:T(8,128)(2,1)S(1)}, u32[]{:S(2)}, u32[]{:S(2)}) collective-permute-start(bf16[128,128]{1,0:T(8,128)(2,1)S(1)} %add_convert_fusion), channel_id=1, source_target_pairs={{0,24},{8,16},{16,8},{24,0},{2,26},{10,18},{18,10},{26,2},{4,28},{... | collective-permute-start | bytes 98312 | tf_op jit(solution)/shard_map/ppermute | solution.py:125
  21.8 5.2 %collective-permute-start.10 = (bf16[128,128]{1,0:T(8,128)(2,1)S(1)}, bf16[128,128]{1,0:T(8,128)(2,1)S(1)}, u32[]{:S(2)}, u32[]{:S(2)}) collective-permute-start(bf16[128,128]{1,0:T(8,128)(2,1)S(1)} %add_convert_fusion), channel_id=1, source_target_pairs={{0,8},{8,0},{16,24},{24,16},{2,10},{10,2},{18,26},{26,18},{4,12},{... | collective-permute-start | bytes 98312 | tf_op jit(solution)/shard_map/ppermute | solution.py:125
  22.1 4.9 %collective-permute-start.9 = (bf16[128,128]{1,0:T(8,128)(2,1)S(1)}, bf16[128,128]{1,0:T(8,128)(2,1)S(1)}, u32[]{:S(2)}, u32[]{:S(2)}) collective-permute-start(bf16[128,128]{1,0:T(8,128)(2,1)S(1)} %add_convert_fusion), channel_id=1, source_target_pairs={{0,16},{8,24},{16,0},{24,8},{2,18},{10,26},{18,2},{26,10},{4,20},{... | collective-permute-start | bytes 98312 | tf_op jit(solution)/shard_map/ppermute | solution.py:125
  24.0 6.7 %collective-permute-start.12 = (bf16[128,128]{1,0:T(8,128)(2,1)S(1)}, bf16[128,128]{1,0:T(8,128)(2,1)S(1)}, u32[]{:S(2)}, u32[]{:S(2)}) collective-permute-start(bf16[128,128]{1,0:T(8,128)(2,1)S(1)} %add_convert_fusion), channel_id=1, source_target_pairs={{0,6},{2,4},{4,2},{6,0},{8,14},{10,12},{12,10},{14,8},{16,22},{18,... | collective-permute-start | bytes 98312 | tf_op jit(solution)/shard_map/ppermute | solution.py:125
  25.9 6.0 %collective-permute-start.11 = (bf16[256,128]{1,0:T(8,128)(2,1)S(1)}, bf16[256,128]{1,0:T(8,128)(2,1)S(1)}, u32[]{:S(2)}, u32[]{:S(2)}) collective-permute-start(bf16[256,128]{1,0:T(8,128)(2,1)S(1)} %pad_maximum_fusion.3), channel_id=1, source_target_pairs={{0,4},{2,6},{4,0},{6,2},{8,12},{10,14},{12,8},{14,10},{16,20},{18,... | collective-permute-start | bytes 196616 | tf_op jit(solution)/shard_map/ppermute | solution.py:125
  27.0 4.8 %copy-start = (bf16[512,172]{0,1:T(8,128)(2,1)S(1)}, bf16[512,172]{0,1:T(8,128)(2,1)}, u32[]{:S(2)}) copy-start(bf16[512,172]{0,1:T(8,128)(2,1)} %param.11) | copy-start | bytes 528388
  27.0 5.8 %collective-permute-start.13 = (bf16[384,128]{1,0:T(8,128)(2,1)S(1)}, bf16[384,128]{1,0:T(8,128)(2,1)S(1)}, u32[]{:S(2)}, u32[]{:S(2)}) collective-permute-start(bf16[384,128]{1,0:T(8,128)(2,1)S(1)} %pad_maximum_fusion.2), channel_id=1, source_target_pairs={{0,6},{2,4},{4,2},{6,0},{8,14},{10,12},{12,10},{14,8},{16,22},{18,... | collective-permute-start | bytes 294920 | tf_op jit(solution)/shard_map/ppermute | solution.py:125
  28.9 5.0 %collective-permute-start.14 = (bf16[512,128]{1,0:T(8,128)(2,1)S(1)}, bf16[512,128]{1,0:T(8,128)(2,1)S(1)}, u32[]{:S(2)}, u32[]{:S(2)}) collective-permute-start(bf16[512,128]{1,0:T(8,128)(2,1)S(1)} %pad_maximum_fusion.refs_0_), channel_id=1, source_target_pairs={{0,2},{2,0},{4,6},{6,4},{8,10},{10,8},{12,14},{14,12},{16,18},{18,... | collective-permute-start | bytes 393224 | tf_op jit(solution)/shard_map/ppermute | solution.py:125
  29.6 4.3 %collective-permute-start.15 = (bf16[256,128]{1,0:T(8,128)(2,1)S(1)}, bf16[256,128]{1,0:T(8,128)(2,1)S(1)}, u32[]{:S(2)}, u32[]{:S(2)}) collective-permute-start(bf16[256,128]{1,0:T(8,128)(2,1)S(1)} %pad_maximum_fusion.4), channel_id=1, source_target_pairs={{0,4},{2,6},{4,0},{6,2},{8,12},{10,14},{12,8},{14,10},{16,20},{18,... | collective-permute-start | bytes 196616 | tf_op jit(solution)/shard_map/ppermute | solution.py:125
  34.8 1.4 %collective-permute-start.16 = (f32[172,128]{1,0:T(8,128)S(1)}, f32[172,128]{1,0:T(8,128)S(1)}, u32[]{:S(2)}, u32[]{:S(2)}) collective-permute-start(f32[172,128]{1,0:T(8,128)S(1)} %get-tuple-element.14), channel_id=1, source_target_pairs={{0,1},{1,0},{2,3},{3,2},{4,5},{5,4},{6,7},{7,6},{8,9},{9,8},{10,11... | collective-permute-start | bytes 264200 | tf_op jit(solution)/shard_map/ppermute | solution.py:155

commit v2 on v1

--- a/solution.py
+++ b/solution.py
@@ -12,7 +12,7 @@
 SMEM = pl.BlockSpec(memory_space=pltpu.SMEM)
 GRANT = pltpu.CompilerParams(vmem_limit_bytes=24 << 20)
 DIRECT = 4
-CFG = {"p": ((3, 2, 1), {2: 1}, (3, 1, 2)), "s": ((3, 1, 2), {3: 1, 2: 2}, (3, 1, 2))}
+CFG = {"p": ((3, 2, 1), {2: 1}, (3, 1, 2)), "s": ((3, 2, 1), {3: 1, 2: 2}, (3, 1, 2))}
 EARLY, MIDDLE, LATE = ((0, True), (1, False), (2, False), (3, False)), ((3, True),), ((1, True), (2, True))
 
 
@@ -118,6 +118,29 @@
         base += size
     for d, out in enumerate(outs):
         out[...] = total[:, d * own : d * own + out.shape[1]]
+
+
+def second_other_kernel(spans, own, high_ref, w_in_t_ref, w_out_t_ref, before_ref, *refs):
+    count = len(spans)
+    pieces, (message_ref, *outs) = refs[:count], refs[count:]
+    message = transform(jnp.concatenate([piece[...] for piece in pieces], 0), w_in_t_ref, w_out_t_ref)
+    message_ref[...] = message
+    for d, out in enumerate(outs, 1):
+        out[...] = before_ref[:, d * own : (d + 1) * own] + late_rows(message, high_ref, slice(d * own, (d + 1) * own), spans)
+
+
+def second_own_kernel(spans, high_ref, before_ref, message_ref, out_ref):
+    own = out_ref.shape[1]
+    out_ref[...] = before_ref[:, :own] + late_rows(message_ref[...], high_ref, slice(0, own), spans)
+
+
+def late_rows(message, high_ref, rows, spans):
+    total, base = 0.0, 0
+    for columns in spans:
+        size = columns.stop - columns.start
+        total = total + times_transposed(message[:, base : base + size], high_ref[rows, columns])
+        base += size
+    return total
 
 
 def hop(value, groups, bits):
@@ -271,7 +294,20 @@
 
         early = second(EARLY, (), False)
         early = second(MIDDLE, early, False)
-        mine, *others = second(LATE, early, True)
+        held, spans = pick_pieces(LATE)
+        size = sum(columns.stop - columns.start for columns in spans)
+        message, *others = call(
+            functools.partial(second_other_kernel, spans, own),
+            [pltpu.VMEM((classes, size), jnp.bfloat16)] + [out_part] * (n_src - 1),
+            0,
+            (high, w_in_t, w_out_t, *early, *held),
+            (),
+            size * (weights + 2 * own * classes),
+        )
+        others = to_owner(others, n_src)
+        mine = call(
+            functools.partial(second_own_kernel, spans), out_part, 0, (high, *early, message), (), 2 * size * own * classes
+        )
     else:
         mine, *others = call(
             functools.partial(second_kernel, len(pieces), tile),
@@ -281,7 +317,8 @@
             scratch,
             depth * (weights + 2 * all_rows * classes),
         )
-    return sum(to_owner(others, n_src), mine).T
+        others = to_owner(others, n_src)
+    return sum(others, mine).T
 
 
 def solution(mesh):

time: 37.1 us -> 37 us (level)
    pallas_call x8 -> x9, Pallas kernels: 4.47 us -> 4.67 us  [call(): pl.pallas_call(kernel, out_shape=outs, in_specs=[SMEM] * n_small + [VMEM]...]
  transfers between devices with their start and end apart: 17 -> 17, of which waited for: 8 -> 8; matrix products, arithmetic and copies ran while one was open for 2% -> 2% of each run, Pallas kernels for 9% -> 10%
where the time goes in v2:
time: 37 us; the launch traced here: 36.8 us
  starting transfers between devices  22.2 us (60%)
  waiting for transfers between devices  6.37 us (17%)
  Pallas kernels  4.67 us (13%)
  local copies, waits for them, and re-layouts  1.95 us (5%)
  between operations  0.83 us (2%)
  other arithmetic  0.72 us (2%)
    ppermute x15, starting transfers between devices, hop(): return lax.ppermute(value, 'tgt', pairs)  22.1 us
    pallas_call x9, Pallas kernels, call(): pl.pallas_call(kernel, out_shape=outs, in_specs=[SMEM] * n_small + [VMEM]...  4.67 us
    ppermute x15, waiting for transfers between devices, hop(): return lax.ppermute(value, 'tgt', pairs)  4.38 us
    ppermute x2, waiting for transfers between devices, to_owner(): moved.append(lax.ppermute(part, 'src', pairs))  1.99 us
    unnamed x11, local copies, waits for them, and re-layouts  1.94 us
  transfers between devices with their start and end apart: 17, of which 8 were waited for; matrix products, arithmetic and copies ran while one was open for 2% of the time, Pallas kernels for 10%

profile of v2, /device:TPU:0, one launch (start us, length us, event | category | flops | bytes accessed | tf_op | source)
XLA Modules:
  0.0 36.8 jit_solution(4723292744679169048)
XLA Ops:
  0.0 5.1 %collective-permute-start = (bf16[128,128]{1,0:T(8,128)(2,1)}, bf16[128,128]{1,0:T(8,128)(2,1)S(1)}, u32[]{:S(2)}, u32[]{:S(2)}) collective-permute-start(bf16[128,128]{1,0:T(8,128)(2,1)} %param.6), channel_id=1, source_target_pairs={{0,24},{8,16},{16,8},{24,0},{2,26},{10,18},{18,10},{26,2},{4,28},{... | collective-permute-start | bytes 98312 | tf_op jit(solution)/shard_map/ppermute | solution.py:148
  5.1 0.0 collective-permute-start.1
  5.1 0.6 %collective-permute-start.2 = (bf16[128,128]{1,0:T(8,128)(2,1)}, bf16[128,128]{1,0:T(8,128)(2,1)S(1)}, u32[]{:S(2)}, u32[]{:S(2)}) collective-permute-start(bf16[128,128]{1,0:T(8,128)(2,1)} %param.6), channel_id=1, source_target_pairs={{0,8},{8,0},{16,24},{24,16},{2,10},{10,2},{18,26},{26,18},{4,12},{... | collective-permute-start | bytes 98312 | tf_op jit(solution)/shard_map/ppermute | solution.py:148
  5.6 1.7 %collective-permute-start.3 = (bf16[128,128]{1,0:T(8,128)(2,1)}, bf16[128,128]{1,0:T(8,128)(2,1)S(1)}, u32[]{:S(2)}, u32[]{:S(2)}) collective-permute-start(bf16[128,128]{1,0:T(8,128)(2,1)} %param.6), channel_id=1, source_target_pairs={{0,4},{2,6},{4,0},{6,2},{8,12},{10,14},{12,8},{14,10},{16,20},{18,... | collective-permute-start | bytes 98312 | tf_op jit(solution)/shard_map/ppermute | solution.py:148
  7.4 0.8 %constant_dynamic-update-slice_fusion.3 = bf16[512,128]{1,0:T(8,128)(2,1)S(1)} fusion(bf16[128,128]{1,0:T(8,128)(2,1)} %param.6), kind=kLoop, calls=%fused_computation.10 | loop fusion | bytes 65536
  8.8 0.0 collective-permute-done
  8.9 1.2 %collective-permute-done.1 = bf16[128,128]{1,0:T(8,128)(2,1)S(1)} collective-permute-done((bf16[128,128]{1,0:T(8,128)(2,1)}, bf16[128,128]{1,0:T(8,128)(2,1)S(1)}, u32[]{:S(2)}, u32[]{:S(2)}) %collective-permute-start.1) | collective-permute-done | bytes 32800 | tf_op jit(solution)/shard_map/ppermute | solution.py:148
  10.1 0.0 copy-start.2
  10.1 0.0 collective-permute-done.2
  10.1 2.5 %collective-permute-start.4 = (bf16[512,128]{1,0:T(8,128)(2,1)S(1)}, bf16[512,128]{1,0:T(8,128)(2,1)S(1)}, u32[]{:S(2)}, u32[]{:S(2)}) collective-permute-start(bf16[512,128]{1,0:T(8,128)(2,1)S(1)} %constant_dynamic-update-slice_fusion.refs_0_), channel_id=1, source_target_pairs={{0,6},{2,4},{4,2},{6,0},{8,14},{10,12},{12,10},{14,8},{16,22},{18,... | collective-permute-start | bytes 393224 | tf_op jit(solution)/shard_map/ppermute | solution.py:148
  12.7 0.5 %collective-permute-start.5 = (bf16[512,128]{1,0:T(8,128)(2,1)S(1)}, bf16[512,128]{1,0:T(8,128)(2,1)S(1)}, u32[]{:S(2)}, u32[]{:S(2)}) collective-permute-start(bf16[512,128]{1,0:T(8,128)(2,1)S(1)} %constant_dynamic-update-slice_fusion.refs_0_), channel_id=1, source_target_pairs={{0,2},{2,0},{4,6},{6,4},{8,10},{10,8},{12,14},{14,12},{16,18},{18,... | collective-permute-start | bytes 393224 | tf_op jit(solution)/shard_map/ppermute | solution.py:148
  13.2 0.0 copy-start.3
  13.2 0.6 %collective-permute-start.6 = (bf16[384,128]{1,0:T(8,128)(2,1)S(1)}, bf16[384,128]{1,0:T(8,128)(2,1)S(1)}, u32[]{:S(2)}, u32[]{:S(2)}) collective-permute-start(bf16[384,128]{1,0:T(8,128)(2,1)S(1)} %pad_maximum_fusion.1), channel_id=1, source_target_pairs={{0,4},{2,6},{4,0},{6,2},{8,12},{10,14},{12,8},{14,10},{16,20},{18,... | collective-permute-start | bytes 294920 | tf_op jit(solution)/shard_map/ppermute | solution.py:148
  13.8 0.1 copy-done.3
  13.9 0.0 copy-done.2
  13.9 0.0 copy-start.1
  13.9 1.0 %copy-done.1 = f32[1,1,8,128,128]{4,3,2,1,0:T(8,128)S(1)} copy-done((f32[1,1,8,128,128]{4,3,2,1,0:T(8,128)S(1)}, f32[1,1,8,128,128]{4,3,2,1,0:T(8,128)}, u32[]{:S(2)}) %copy-start.1) | copy-done | bytes 524312
  14.9 0.9 %shard_map.64 = (bf16[256,2048]{1,0:T(8,128)(2,1)S(1)}, bf16[256,2048]{1,0:T(8,128)(2,1)S(1)}, bf16[512,128]{1,0:T(8,128)(2,1)S(1)}) custom-call(s32[8]{0:T(128)S(1)} %get-tuple-element.16.code_ref, s32[8]{0:T(128)S(1)} %get-tuple-element.15.spot_ref, f32[8,128,128]{2,1,0:T(8,128)S(1)} %bitcast.26, bf16[128,512]{1,0:T(8,128)(2,1)S(1)} %copy-done.2), custom_call_target="tpu_custom_call" | custom-call | bytes 1048576 | tf_op jit(solution)/shard_map/pallas_call | solution.py:213
  15.9 0.0 collective-permute-done.3.refs_1_
  15.9 0.3 shard_map.65.refs_0_
  16.2 0.1 collective-permute-done.4.refs_1_
  16.3 0.3 shard_map.66.refs_0_
  16.6 1.3 %collective-permute-done.6.refs_2_ = bf16[384,128]{1,0:T(8,128)(2,1)S(1)} collective-permute-done((bf16[384,128]{1,0:T(8,128)(2,1)S(1)}, bf16[384,128]{1,0:T(8,128)(2,1)S(1)}, u32[]{:S(2)}, u32[]{:S(2)}) %collective-permute-start.6) | collective-permute-done | bytes 98336 | tf_op jit(solution)/shard_map/ppermute | solution.py:148
  17.9 0.0 collective-permute-done.5.refs_1_
  17.9 0.3 shard_map.68
  18.2 0.1 collective-permute-start.7
  18.3 0.3 shard_map.67
  18.5 1.0 %collective-permute-done.7 = f32[128,128]{1,0:T(8,128)S(1)} collective-permute-done((f32[128,128]{1,0:T(8,128)S(1)}, f32[128,128]{1,0:T(8,128)S(1)}, u32[]{:S(2)}, u32[]{:S(2)}) %collective-permute-start.7) | collective-permute-done | bytes 65568 | tf_op jit(solution)/shard_map/ppermute | solution.py:178
  19.5 2.2 %collective-permute-start.8 = (bf16[128,128]{1,0:T(8,128)(2,1)S(1)}, bf16[128,128]{1,0:T(8,128)(2,1)S(1)}, u32[]{:S(2)}, u32[]{:S(2)}) collective-permute-start(bf16[128,128]{1,0:T(8,128)(2,1)S(1)} %add_convert_fusion), channel_id=1, source_target_pairs={{0,24},{8,16},{16,8},{24,0},{2,26},{10,18},{18,10},{26,2},{4,28},{... | collective-permute-start | bytes 98312 | tf_op jit(solution)/shard_map/ppermute | solution.py:148
  21.8 0.3 collective-permute-start.10
  22.1 1.9 %collective-permute-start.9 = (bf16[128,128]{1,0:T(8,128)(2,1)S(1)}, bf16[128,128]{1,0:T(8,128)(2,1)S(1)}, u32[]{:S(2)}, u32[]{:S(2)}) collective-permute-start(bf16[128,128]{1,0:T(8,128)(2,1)S(1)} %add_convert_fusion), channel_id=1, source_target_pairs={{0,16},{8,24},{16,0},{24,8},{2,18},{10,26},{18,2},{26,10},{4,20},{... | collective-permute-start | bytes 98312 | tf_op jit(solution)/shard_map/ppermute | solution.py:148
  24.0 1.9 %collective-permute-start.12 = (bf16[128,128]{1,0:T(8,128)(2,1)S(1)}, bf16[128,128]{1,0:T(8,128)(2,1)S(1)}, u32[]{:S(2)}, u32[]{:S(2)}) collective-permute-start(bf16[128,128]{1,0:T(8,128)(2,1)S(1)} %add_convert_fusion), channel_id=1, source_target_pairs={{0,6},{2,4},{4,2},{6,0},{8,14},{10,12},{12,10},{14,8},{16,22},{18,... | collective-permute-start | bytes 98312 | tf_op jit(solution)/shard_map/ppermute | solution.py:148
  25.9 0.0 collective-permute-done.8
  25.9 1.1 %collective-permute-start.11 = (bf16[256,128]{1,0:T(8,128)(2,1)S(1)}, bf16[256,128]{1,0:T(8,128)(2,1)S(1)}, u32[]{:S(2)}, u32[]{:S(2)}) collective-permute-start(bf16[256,128]{1,0:T(8,128)(2,1)S(1)} %pad_maximum_fusion.3), channel_id=1, source_target_pairs={{0,4},{2,6},{4,0},{6,2},{8,12},{10,14},{12,8},{14,10},{16,20},{18,... | collective-permute-start | bytes 196616 | tf_op jit(solution)/shard_map/ppermute | solution.py:148
  27.0 0.0 collective-permute-done.10
  27.0 0.0 collective-permute-done.9
  27.0 0.0 copy-start
  27.0 1.9 %collective-permute-start.13 = (bf16[384,128]{1,0:T(8,128)(2,1)S(1)}, bf16[384,128]{1,0:T(8,128)(2,1)S(1)}, u32[]{:S(2)}, u32[]{:S(2)}) collective-permute-start(bf16[384,128]{1,0:T(8,128)(2,1)S(1)} %pad_maximum_fusion.2), channel_id=1, source_target_pairs={{0,6},{2,4},{4,2},{6,0},{8,14},{10,12},{12,10},{14,8},{16,22},{18,... | collective-permute-start | bytes 294920 | tf_op jit(solution)/shard_map/ppermute | solution.py:148
  28.9 0.7 %collective-permute-start.14 = (bf16[512,128]{1,0:T(8,128)(2,1)S(1)}, bf16[512,128]{1,0:T(8,128)(2,1)S(1)}, u32[]{:S(2)}, u32[]{:S(2)}) collective-permute-start(bf16[512,128]{1,0:T(8,128)(2,1)S(1)} %pad_maximum_fusion.refs_0_), channel_id=1, source_target_pairs={{0,2},{2,0},{4,6},{6,4},{8,10},{10,8},{12,14},{14,12},{16,18},{18,... | collective-permute-start | bytes 393224 | tf_op jit(solution)/shard_map/ppermute | solution.py:148
  29.6 1.0 %collective-permute-start.15 = (bf16[256,128]{1,0:T(8,128)(2,1)S(1)}, bf16[256,128]{1,0:T(8,128)(2,1)S(1)}, u32[]{:S(2)}, u32[]{:S(2)}) collective-permute-start(bf16[256,128]{1,0:T(8,128)(2,1)S(1)} %pad_maximum_fusion.4), channel_id=1, source_target_pairs={{0,4},{2,6},{4,0},{6,2},{8,12},{10,14},{12,8},{14,10},{16,20},{18,... | collective-permute-start | bytes 196616 | tf_op jit(solution)/shard_map/ppermute | solution.py:148
  30.7 0.0 collective-permute-done.12.refs_2_
  30.7 1.2 %collective-permute-done.11.refs_1_ = bf16[256,128]{1,0:T(8,128)(2,1)S(1)} collective-permute-done((bf16[256,128]{1,0:T(8,128)(2,1)S(1)}, bf16[256,128]{1,0:T(8,128)(2,1)S(1)}, u32[]{:S(2)}, u32[]{:S(2)}) %collective-permute-start.11) | collective-permute-done | bytes 65568 | tf_op jit(solution)/shard_map/ppermute | solution.py:148
  31.9 0.0 copy-done
  31.9 1.0 %shard_map.69.refs_0_ = f32[172,256]{1,0:T(8,128)S(1)} custom-call(bf16[256,2048]{1,0:T(8,128)(2,1)S(1)} %get-tuple-element.10.high_ref, bf16[512,128]{1,0:T(8,128)(2,1)S(1)} %get-tuple-element.11.w_in_t_ref, bf16[172,512]{1,0:T(8,128)(2,1)S(1)} %bitcast.23, bf16[512,128]{1,0:T(8,128)(2,1)S(1)} %pad_maximum_fusion.refs_0_, ...), custom_call_target="tpu_custom_call" | custom-call | flops 202375168 | bytes 1048576 | tf_op jit(solution)/shard_map/pallas_call | solution.py:213
  32.8 0.0 collective-permute-done.13.refs_1_
  32.9 0.6 %shard_map.70.before_ref = f32[172,256]{1,0:T(8,128)S(1)} custom-call(bf16[256,2048]{1,0:T(8,128)(2,1)S(1)} %get-tuple-element.10.high_ref, bf16[512,128]{1,0:T(8,128)(2,1)S(1)} %get-tuple-element.11.w_in_t_ref, bf16[172,512]{1,0:T(8,128)(2,1)S(1)} %bitcast.24, f32[172,256]{1,0:T(8,128)S(1)} %shard_map.69.refs_0_, ...), custom_call_target="tpu_custom_call" | custom-call | flops 202375168 | bytes 1048576 | tf_op jit(solution)/shard_map/pallas_call | solution.py:213
  33.5 0.4 %collective-permute-done.15.refs_1_ = bf16[256,128]{1,0:T(8,128)(2,1)S(1)} collective-permute-done((bf16[256,128]{1,0:T(8,128)(2,1)S(1)}, bf16[256,128]{1,0:T(8,128)(2,1)S(1)}, u32[]{:S(2)}, u32[]{:S(2)}) %collective-permute-start.15) | collective-permute-done | bytes 65568 | tf_op jit(solution)/shard_map/ppermute | solution.py:148
  33.9 0.1 collective-permute-done.14.refs_0_
  34.0 0.8 %shard_map.71 = (bf16[172,768]{1,0:T(8,128)(2,1)S(1)}, f32[172,128]{1,0:T(8,128)S(1)}) custom-call(bf16[256,2048]{1,0:T(8,128)(2,1)S(1)} %get-tuple-element.10.high_ref, bf16[512,128]{1,0:T(8,128)(2,1)S(1)} %get-tuple-element.11.w_in_t_ref, bf16[172,512]{1,0:T(8,128)(2,1)S(1)} %bitcast.25, f32[172,256]{1,0:T(8,128)S(1)} %shard_map.70.before_ref, ...), custom_call_target="tpu_custom_call" | custom-call | flops 269746176 | bytes 1048576 | tf_op jit(solution)/shard_map/pallas_call | solution.py:213
  34.8 0.1 collective-permute-start.16
  34.8 0.2 shard_map.72
  35.1 1.0 %collective-permute-done.16 = f32[172,128]{1,0:T(8,128)S(1)} collective-permute-done((f32[172,128]{1,0:T(8,128)S(1)}, f32[172,128]{1,0:T(8,128)S(1)}, u32[]{:S(2)}, u32[]{:S(2)}) %collective-permute-start.16) | collective-permute-done | bytes 88096 | tf_op jit(solution)/shard_map/ppermute | solution.py:178
  36.1 0.6 %add_bitcast_fusion = f32[128,172]{0,1:T(8,128)} fusion(f32[172,128]{1,0:T(8,128)S(1)} %shard_map.72, f32[172,128]{1,0:T(8,128)S(1)} %collective-permute-done.16), kind=kLoop, calls=%fused_computation.3 | loop fusion | flops 22016 | bytes 264192 | tf_op jit(solution)/shard_map/transpose | solution.py:321
  (10 shorter events, 0.1 us)
Async XLA Ops:
  0.0 8.8 %collective-permute-start = (bf16[128,128]{1,0:T(8,128)(2,1)}, bf16[128,128]{1,0:T(8,128)(2,1)S(1)}, u32[]{:S(2)}, u32[]{:S(2)}) collective-permute-start(bf16[128,128]{1,0:T(8,128)(2,1)} %param.6), channel_id=1, source_target_pairs={{0,24},{8,16},{16,8},{24,0},{2,26},{10,18},{18,10},{26,2},{4,28},{... | collective-permute-start | bytes 98312 | tf_op jit(solution)/shard_map/ppermute | solution.py:148
  5.1 5.0 %collective-permute-start.1 = (bf16[128,128]{1,0:T(8,128)(2,1)}, bf16[128,128]{1,0:T(8,128)(2,1)S(1)}, u32[]{:S(2)}, u32[]{:S(2)}) collective-permute-start(bf16[128,128]{1,0:T(8,128)(2,1)} %param.6), channel_id=1, source_target_pairs={{0,16},{8,24},{16,0},{24,8},{2,18},{10,26},{18,2},{26,10},{4,20},{... | collective-permute-start | bytes 98312 | tf_op jit(solution)/shard_map/ppermute | solution.py:148
  5.1 5.0 %collective-permute-start.2 = (bf16[128,128]{1,0:T(8,128)(2,1)}, bf16[128,128]{1,0:T(8,128)(2,1)S(1)}, u32[]{:S(2)}, u32[]{:S(2)}) collective-permute-start(bf16[128,128]{1,0:T(8,128)(2,1)} %param.6), channel_id=1, source_target_pairs={{0,8},{8,0},{16,24},{24,16},{2,10},{10,2},{18,26},{26,18},{4,12},{... | collective-permute-start | bytes 98312 | tf_op jit(solution)/shard_map/ppermute | solution.py:148
  5.6 10.2 %collective-permute-start.3 = (bf16[128,128]{1,0:T(8,128)(2,1)}, bf16[128,128]{1,0:T(8,128)(2,1)S(1)}, u32[]{:S(2)}, u32[]{:S(2)}) collective-permute-start(bf16[128,128]{1,0:T(8,128)(2,1)} %param.6), channel_id=1, source_target_pairs={{0,4},{2,6},{4,0},{6,2},{8,12},{10,14},{12,8},{14,10},{16,20},{18,... | collective-permute-start | bytes 98312 | tf_op jit(solution)/shard_map/ppermute | solution.py:148
  10.1 3.8 %copy-start.2 = (bf16[128,512]{1,0:T(8,128)(2,1)S(1)}, bf16[128,512]{1,0:T(8,128)(2,1)}, u32[]{:S(2)}) copy-start(bf16[128,512]{1,0:T(8,128)(2,1)} %w_in_ref.1) | copy-start | bytes 393220
  10.1 6.2 %collective-permute-start.4 = (bf16[512,128]{1,0:T(8,128)(2,1)S(1)}, bf16[512,128]{1,0:T(8,128)(2,1)S(1)}, u32[]{:S(2)}, u32[]{:S(2)}) collective-permute-start(bf16[512,128]{1,0:T(8,128)(2,1)S(1)} %constant_dynamic-update-slice_fusion.refs_0_), channel_id=1, source_target_pairs={{0,6},{2,4},{4,2},{6,0},{8,14},{10,12},{12,10},{14,8},{16,22},{18,... | collective-permute-start | bytes 393224 | tf_op jit(solution)/shard_map/ppermute | solution.py:148
  12.7 5.2 %collective-permute-start.5 = (bf16[512,128]{1,0:T(8,128)(2,1)S(1)}, bf16[512,128]{1,0:T(8,128)(2,1)S(1)}, u32[]{:S(2)}, u32[]{:S(2)}) collective-permute-start(bf16[512,128]{1,0:T(8,128)(2,1)S(1)} %constant_dynamic-update-slice_fusion.refs_0_), channel_id=1, source_target_pairs={{0,2},{2,0},{4,6},{6,4},{8,10},{10,8},{12,14},{14,12},{16,18},{18,... | collective-permute-start | bytes 393224 | tf_op jit(solution)/shard_map/ppermute | solution.py:148
  13.2 0.7 %copy-start.3 = (s32[1,1,8]{2,1,0:T(1,128)S(1)}, s32[1,1,8]{2,1,0:T(1,128)}, u32[]{:S(2)}) copy-start(s32[1,1,8]{2,1,0:T(1,128)} %param.7) | copy-start | bytes 100
  13.2 4.7 %collective-permute-start.6 = (bf16[384,128]{1,0:T(8,128)(2,1)S(1)}, bf16[384,128]{1,0:T(8,128)(2,1)S(1)}, u32[]{:S(2)}, u32[]{:S(2)}) collective-permute-start(bf16[384,128]{1,0:T(8,128)(2,1)S(1)} %pad_maximum_fusion.1), channel_id=1, source_target_pairs={{0,4},{2,6},{4,0},{6,2},{8,12},{10,14},{12,8},{14,10},{16,20},{18,... | collective-permute-start | bytes 294920 | tf_op jit(solution)/shard_map/ppermute | solution.py:148
  13.9 1.0 %copy-start.1 = (f32[1,1,8,128,128]{4,3,2,1,0:T(8,128)S(1)}, f32[1,1,8,128,128]{4,3,2,1,0:T(8,128)}, u32[]{:S(2)}) copy-start(f32[1,1,8,128,128]{4,3,2,1,0:T(8,128)} %param.9) | copy-start | bytes 1572868
  18.2 1.3 %collective-permute-start.7 = (f32[128,128]{1,0:T(8,128)S(1)}, f32[128,128]{1,0:T(8,128)S(1)}, u32[]{:S(2)}, u32[]{:S(2)}) collective-permute-start(f32[128,128]{1,0:T(8,128)S(1)} %shard_map.68), channel_id=1, source_target_pairs={{0,1},{1,0},{2,3},{3,2},{4,5},{5,4},{6,7},{7,6},{8,9},{9,8},{10,11... | collective-permute-start | bytes 196616 | tf_op jit(solution)/shard_map/ppermute | solution.py:178
  19.5 6.4 %collective-permute-start.8 = (bf16[128,128]{1,0:T(8,128)(2,1)S(1)}, bf16[128,128]{1,0:T(8,128)(2,1)S(1)}, u32[]{:S(2)}, u32[]{:S(2)}) collective-permute-start(bf16[128,128]{1,0:T(8,128)(2,1)S(1)} %add_convert_fusion), channel_id=1, source_target_pairs={{0,24},{8,16},{16,8},{24,0},{2,26},{10,18},{18,10},{26,2},{4,28},{... | collective-permute-start | bytes 98312 | tf_op jit(solution)/shard_map/ppermute | solution.py:148
  21.8 5.2 %collective-permute-start.10 = (bf16[128,128]{1,0:T(8,128)(2,1)S(1)}, bf16[128,128]{1,0:T(8,128)(2,1)S(1)}, u32[]{:S(2)}, u32[]{:S(2)}) collective-permute-start(bf16[128,128]{1,0:T(8,128)(2,1)S(1)} %add_convert_fusion), channel_id=1, source_target_pairs={{0,8},{8,0},{16,24},{24,16},{2,10},{10,2},{18,26},{26,18},{4,12},{... | collective-permute-start | bytes 98312 | tf_op jit(solution)/shard_map/ppermute | solution.py:148
  22.1 4.9 %collective-permute-start.9 = (bf16[128,128]{1,0:T(8,128)(2,1)S(1)}, bf16[128,128]{1,0:T(8,128)(2,1)S(1)}, u32[]{:S(2)}, u32[]{:S(2)}) collective-permute-start(bf16[128,128]{1,0:T(8,128)(2,1)S(1)} %add_convert_fusion), channel_id=1, source_target_pairs={{0,16},{8,24},{16,0},{24,8},{2,18},{10,26},{18,2},{26,10},{4,20},{... | collective-permute-start | bytes 98312 | tf_op jit(solution)/shard_map/ppermute | solution.py:148
  24.0 6.7 %collective-permute-start.12 = (bf16[128,128]{1,0:T(8,128)(2,1)S(1)}, bf16[128,128]{1,0:T(8,128)(2,1)S(1)}, u32[]{:S(2)}, u32[]{:S(2)}) collective-permute-start(bf16[128,128]{1,0:T(8,128)(2,1)S(1)} %add_convert_fusion), channel_id=1, source_target_pairs={{0,6},{2,4},{4,2},{6,0},{8,14},{10,12},{12,10},{14,8},{16,22},{18,... | collective-permute-start | bytes 98312 | tf_op jit(solution)/shard_map/ppermute | solution.py:148
  25.9 6.0 %collective-permute-start.11 = (bf16[256,128]{1,0:T(8,128)(2,1)S(1)}, bf16[256,128]{1,0:T(8,128)(2,1)S(1)}, u32[]{:S(2)}, u32[]{:S(2)}) collective-permute-start(bf16[256,128]{1,0:T(8,128)(2,1)S(1)} %pad_maximum_fusion.3), channel_id=1, source_target_pairs={{0,4},{2,6},{4,0},{6,2},{8,12},{10,14},{12,8},{14,10},{16,20},{18,... | collective-permute-start | bytes 196616 | tf_op jit(solution)/shard_map/ppermute | solution.py:148
  27.0 4.8 %copy-start = (bf16[512,172]{0,1:T(8,128)(2,1)S(1)}, bf16[512,172]{0,1:T(8,128)(2,1)}, u32[]{:S(2)}) copy-start(bf16[512,172]{0,1:T(8,128)(2,1)} %param.11) | copy-start | bytes 528388
  27.0 5.8 %collective-permute-start.13 = (bf16[384,128]{1,0:T(8,128)(2,1)S(1)}, bf16[384,128]{1,0:T(8,128)(2,1)S(1)}, u32[]{:S(2)}, u32[]{:S(2)}) collective-permute-start(bf16[384,128]{1,0:T(8,128)(2,1)S(1)} %pad_maximum_fusion.2), channel_id=1, source_target_pairs={{0,6},{2,4},{4,2},{6,0},{8,14},{10,12},{12,10},{14,8},{16,22},{18,... | collective-permute-start | bytes 294920 | tf_op jit(solution)/shard_map/ppermute | solution.py:148
  28.9 5.0 %collective-permute-start.14 = (bf16[512,128]{1,0:T(8,128)(2,1)S(1)}, bf16[512,128]{1,0:T(8,128)(2,1)S(1)}, u32[]{:S(2)}, u32[]{:S(2)}) collective-permute-start(bf16[512,128]{1,0:T(8,128)(2,1)S(1)} %pad_maximum_fusion.refs_0_), channel_id=1, source_target_pairs={{0,2},{2,0},{4,6},{6,4},{8,10},{10,8},{12,14},{14,12},{16,18},{18,... | collective-permute-start | bytes 393224 | tf_op jit(solution)/shard_map/ppermute | solution.py:148
  29.6 4.3 %collective-permute-start.15 = (bf16[256,128]{1,0:T(8,128)(2,1)S(1)}, bf16[256,128]{1,0:T(8,128)(2,1)S(1)}, u32[]{:S(2)}, u32[]{:S(2)}) collective-permute-start(bf16[256,128]{1,0:T(8,128)(2,1)S(1)} %pad_maximum_fusion.4), channel_id=1, source_target_pairs={{0,4},{2,6},{4,0},{6,2},{8,12},{10,14},{12,8},{14,10},{16,20},{18,... | collective-permute-start | bytes 196616 | tf_op jit(solution)/shard_map/ppermute | solution.py:148
  34.8 1.4 %collective-permute-start.16 = (f32[172,128]{1,0:T(8,128)S(1)}, f32[172,128]{1,0:T(8,128)S(1)}, u32[]{:S(2)}, u32[]{:S(2)}) collective-permute-start(f32[172,128]{1,0:T(8,128)S(1)} %get-tuple-element.14), channel_id=1, source_target_pairs={{0,1},{1,0},{2,3},{3,2},{4,5},{5,4},{6,7},{7,6},{8,9},{9,8},{10,11... | collective-permute-start | bytes 264200 | tf_op jit(solution)/shard_map/ppermute | solution.py:178
